TPU v7x, 32 devices: a whole 2x2x4 slice. The times are simulated.
32 devices in a mesh: dp: 8 (over y, x, core), mp: 4 (over z).
Axes of the slice: x: 2, y: 2, z: 4, core: 2. Of those that a mesh axis runs over, the one named last changes fastest.
Arguments:
- tokens: bfloat16 [16384, 768], P(('dp', 'mp')), may hold values from -6 to 6
- segments: int32 [32, 512], P('dp'), may hold values from 0 to 5, never falling along the last dimension, each value on 1 to 256 neighbouring positions
- w_query: bfloat16 [768, 768], P(None, 'mp'), may hold values from -0.21875 to 0.21875
- b_query: bfloat16 [768], P('mp'), may hold values from -3 to 3
- w_key: bfloat16 [768, 768], P(None, 'mp'), may hold values from -0.21875 to 0.21875
- w_value: bfloat16 [768, 768], P(None, 'mp'), may hold values from -0.21875 to 0.21875
- b_value: bfloat16 [768], P('mp'), may hold values from -3 to 3
- w_out: bfloat16 [768, 768], P('mp'), may hold values from -0.625 to 0.625
- b_out: bfloat16 [768], replicated, may hold values from -3 to 3
- first_norm_gain: bfloat16 [768], replicated, may hold values from 0.099609375 to 1.8984375
- first_norm_bias: bfloat16 [768], replicated, may hold values from -3 to 3
- w_up: bfloat16 [768, 3072], P(None, 'mp'), may hold values from -0.21875 to 0.21875
- b_up: bfloat16 [3072], P('mp'), may hold values from -3 to 3
- w_down: bfloat16 [3072, 768], P('mp'), may hold values from -0.109375 to 0.109375
- b_down: bfloat16 [768], replicated, may hold values from -3 to 3
- second_norm_gain: bfloat16 [768], replicated, may hold values from 0.099609375 to 1.8984375
- second_norm_bias: bfloat16 [768], replicated, may hold values from -3 to 3
- output_gradient: bfloat16 [16384, 768], P(('dp', 'mp')), may hold values from -6 to 6
Outputs:
- out_tokens: bfloat16 [16384, 768], P(('dp', 'mp'))
- grad_tokens: bfloat16 [16384, 768], P(('dp', 'mp'))
- grad_w_query: float32 [768, 768], P(None, 'mp')
- grad_b_query: float32 [768], P('mp')
- grad_w_key: float32 [768, 768], P(None, 'mp')
- grad_w_value: float32 [768, 768], P(None, 'mp')
- grad_b_value: float32 [768], P('mp')
- grad_w_out: float32 [768, 768], P('mp')
- grad_b_out: float32 [768], replicated
- grad_norm1_gain: float32 [768], replicated
- grad_norm1_bias: float32 [768], replicated
- grad_w_up: float32 [768, 3072], P(None, 'mp')
- grad_b_up: float32 [3072], P('mp')
- grad_w_down: float32 [3072, 768], P('mp')
- grad_b_down: float32 [768], replicated
- grad_norm2_gain: float32 [768], replicated
- grad_norm2_bias: float32 [768], replicated
Inputs may be any that keep to these rules, and one draw needn't show every extreme that they name: `segments`: document numbers never fall along a sequence; a document holds 1 to 256 positions, and in every sequence one holds exactly 256.
All inputs are finite; a program needn't handle non-finite values.
Results may differ from a plain program's by a relative error of at most 0.015.
Values may be sent and summed in bfloat16 or wider, within the bound.
No kernel may reach another device: no remote copies, remote signals or barrier semaphores. Data moves between devices by JAX's collectives and lax.ppermute only.
A program may use at most 128 MiB of HBM per device.

v0:
```python
import jax
import jax.numpy as jnp
from jax import lax
from jax.sharding import PartitionSpec as P

HEAD_DIM = 64
EPS = 1e-05
INV_ROOT_TWO = 0.7071067811865476
INV_ROOT_TWO_PI = 0.3989422804014327
CUBE = 8
f32 = jnp.float32
bf16 = jnp.bfloat16


def dot(left, right, dims):
    return lax.dot_general(
        left, right, ((dims[:1], dims[1:]), ((), ())), preferred_element_type=f32
    )


def norm_forward(values, gain, bias):
    average = jnp.mean(values, -1, keepdims=True)
    centered = values - average
    spread = jnp.mean(centered * centered, -1, keepdims=True)
    rstd = lax.rsqrt(spread + EPS)
    xhat = centered * rstd
    return (xhat * gain + bias, xhat, rstd)


def norm_backward(grad, xhat, rstd, gain):
    scaled = grad * gain
    result = rstd * (
        scaled
        - jnp.mean(scaled, -1, keepdims=True)
        - xhat * jnp.mean(scaled * xhat, -1, keepdims=True)
    )
    return (result, jnp.sum(grad * xhat, 0), jnp.sum(grad, 0))


def gelu_parts(v):
    phi = 0.5 * (1.0 + lax.erf(v * INV_ROOT_TWO))
    return (v * phi, phi + v * jnp.exp(-0.5 * v * v) * INV_ROOT_TWO_PI)


class Links:

    def __init__(self, dp, mp):
        self.dp, self.mp = (dp, mp)
        self.index = lax.axis_index("dp")
        self.place = self.index % CUBE

    def shift(self, x, by):
        return lax.ppermute(x, "mp", [(i, (i + by) % self.mp) for i in range(self.mp)])

    def flip(self, x, bit):
        return lax.ppermute(x, "dp", [(i, i ^ bit) for i in range(self.dp)])

    def spread(self, piece):
        half = piece.shape[0] // 2
        over_x = self.flip(piece, 2)
        over_y = self.flip(piece, 4)
        diag_a = self.flip(over_x[:half], 4)
        diag_b = self.flip(over_y[half:], 2)
        diag = jnp.concatenate([diag_a, diag_b])
        even = [piece, over_x, over_y, diag]
        odd = [self.flip(part, 1) for part in even]
        return [even[0], odd[0], even[1], odd[1], even[2], odd[2], even[3], odd[3]]

    def ordered(self, parts):
        stacked = jnp.stack(parts)
        return jnp.stack(
            [
                lax.dynamic_index_in_dim(stacked, self.place ^ q, 0, keepdims=False)
                for q in range(CUBE)
            ]
        )

    def gather(self, shard):
        rows, cols = shard.shape
        step = rows // CUBE
        piece = lax.dynamic_slice_in_dim(shard, self.place * step, step, 0)
        others = jnp.concatenate([self.shift(piece, s) for s in range(1, self.mp)])
        whole = self.ordered(self.spread(others)).reshape(CUBE, self.mp - 1, step, cols)
        whole = whole.transpose(1, 0, 2, 3).reshape(self.mp - 1, rows, cols)
        return [shard] + [whole[s] for s in range(self.mp - 1)]

    def reduce(self, blocks):
        rows, cols = blocks[0].shape
        step = rows // CUBE
        stacked = jnp.stack(blocks).reshape(self.mp, CUBE, step, cols)
        rel = [
            lax.dynamic_index_in_dim(stacked, self.place ^ r, 1, keepdims=False).astype(bf16)
            for r in range(CUBE)
        ]
        other = self.flip(jnp.stack(rel[1::2]), 1)
        add = lambda *terms: sum((t.astype(f32) for t in terms)).astype(bf16)
        own, to_x, to_y, to_diag = [add(rel[2 * i], other[i]) for i in range(4)]
        cut = self.mp // 2
        a, b = (slice(0, cut), slice(cut, self.mp))
        from_x = self.flip(jnp.stack([to_diag[a], to_x[a]]), 2)
        from_y = self.flip(jnp.stack([to_diag[b], to_y[b]]), 4)
        last_x = self.flip(add(to_x[b], from_y[0]), 2)
        last_y = self.flip(add(to_y[a], from_x[0]), 4)
        own = jnp.concatenate([add(own[a], from_x[1], last_y), add(own[b], last_x, from_y[1])])
        terms = [own[0]] + [self.shift(own[s], -s) for s in range(1, self.mp)]
        total = sum((t.astype(f32) for t in terms))
        if self.dp > CUBE:
            groups = [[g * CUBE + i for g in range(self.dp // CUBE)] for i in range(CUBE)]
            total = lax.psum(total, "dp", axis_index_groups=groups)
        return total


def scores_of(queries, key_rows, same_doc):
    scores = jnp.einsum("qhd,khd->hqk", queries, key_rows, preferred_element_type=f32)
    return jnp.where(same_doc[None], scores * HEAD_DIM ** (-0.5), -1e30)


def attend_forward(queries, key_rows, value_rows, same_doc):
    scores = scores_of(queries, key_rows, same_doc)
    highest = jnp.max(scores, -1, keepdims=True)
    expd = jnp.exp(scores - highest)
    totals = jnp.sum(expd, -1, keepdims=True)
    probs = (expd / totals).astype(bf16)
    context = jnp.einsum("hqk,khd->qhd", probs, value_rows, preferred_element_type=f32)
    return (context.astype(bf16), (highest + jnp.log(totals))[..., 0])


def attend_backward(queries, key_rows, value_rows, g_context, log_sums, same_doc):
    scores = scores_of(queries, key_rows, same_doc)
    probs = jnp.exp(scores - log_sums[..., None])
    g_value = jnp.einsum("hqk,qhd->khd", probs.astype(bf16), g_context, preferred_element_type=f32)
    g_probs = jnp.einsum("qhd,khd->hqk", g_context, value_rows, preferred_element_type=f32)
    centre = jnp.sum(probs * g_probs, -1, keepdims=True)
    g_scores = (probs * (g_probs - centre)).astype(bf16)
    scale = HEAD_DIM ** (-0.5)
    g_query = scale * jnp.einsum("hqk,khd->qhd", g_scores, key_rows, preferred_element_type=f32)
    g_key = scale * jnp.einsum("hqk,qhd->khd", g_scores, queries, preferred_element_type=f32)
    return (g_query.astype(bf16), g_key.astype(bf16), g_value.astype(bf16))


def per_device(
    dp,
    mp,
    tokens,
    segments,
    w_query,
    b_query,
    w_key,
    w_value,
    b_value,
    w_out,
    b_out,
    first_norm_gain,
    first_norm_bias,
    w_up,
    b_up,
    w_down,
    b_down,
    second_norm_gain,
    second_norm_bias,
    output_gradient,
):
    links = Links(dp, mp)
    slots = range(mp)
    rows, width = tokens.shape
    part = w_query.shape[1]
    heads = part // HEAD_DIM
    gain1, bias1 = (first_norm_gain.astype(f32), first_norm_bias.astype(f32))
    gain2, bias2 = (second_norm_gain.astype(f32), second_norm_bias.astype(f32))
    segment = lax.dynamic_index_in_dim(segments, lax.axis_index("mp"), 0, keepdims=False)
    same_doc = segment[:, None] == segment[None, :]
    mixed = jnp.concatenate([w_query, w_key, w_value, w_out.T], axis=1)
    a_blocks = links.gather(mixed)
    vectors = jnp.concatenate([b_query, b_value, b_up])
    vectors = [vectors] + [links.shift(vectors, s) for s in range(1, mp)]
    bq = [v[:part].astype(f32) for v in vectors]
    bv = [v[part : 2 * part].astype(f32) for v in vectors]
    bu = [v[2 * part :].astype(f32) for v in vectors]
    u_blocks = links.gather(w_up)
    d_blocks = links.gather(w_down)
    by_head = lambda t: t.reshape(rows, heads, HEAD_DIM)
    by_rows = lambda t: t.reshape(rows, heads * HEAD_DIM)
    saved = []
    attended = tokens.astype(f32) + b_out.astype(f32)
    for s in slots:
        mix = dot(tokens, a_blocks[s][:, : 3 * part], (1, 0))
        q = by_head((mix[:, :part] + bq[s]).astype(bf16))
        k = by_head(mix[:, part : 2 * part].astype(bf16))
        v = by_head((mix[:, 2 * part :] + bv[s]).astype(bf16))
        context, sums = attend_forward(q, k, v, same_doc)
        context = by_rows(context)
        saved.append((q, k, v, context, sums))
        attended = attended + dot(context, a_blocks[s][:, 3 * part :], (1, 1))
    normed, xhat1, rstd1 = norm_forward(attended, gain1, bias1)
    normed_low = normed.astype(bf16)
    acts, slopes = ([], [])
    summed = normed + b_down.astype(f32)
    for s in slots:
        act, slope = gelu_parts(dot(normed_low, u_blocks[s], (1, 0)) + bu[s])
        acts.append(act.astype(bf16))
        slopes.append(slope)
        summed = summed + dot(acts[s], d_blocks[s], (1, 0))
    out_tokens, xhat2, rstd2 = norm_forward(summed, gain2, bias2)
    g_summed, g_gain2, g_bias2 = norm_backward(output_gradient.astype(f32), xhat2, rstd2, gain2)
    g_b_down = jnp.sum(g_summed, 0)
    g_low = g_summed.astype(bf16)
    piece_d = links.reduce([dot(acts[s], g_low, (0, 0)) for s in slots])
    g_pre = [(dot(g_low, d_blocks[s], (1, 1)) * slopes[s]).astype(bf16) for s in slots]
    piece_u = links.reduce([dot(normed_low, g_pre[s], (0, 0)) for s in slots])
    g_b_up = [jnp.sum(g.astype(f32), 0) for g in g_pre]
    g_normed = g_summed
    for s in slots:
        g_normed = g_normed + dot(g_pre[s], u_blocks[s], (1, 1))
    g_attended, g_gain1, g_bias1 = norm_backward(g_normed, xhat1, rstd1, gain1)
    g_b_out = jnp.sum(g_attended, 0)
    ga_low = g_attended.astype(bf16)
    g_tokens = g_attended
    g_mixed, g_bq, g_bv = ([], [], [])
    for s in slots:
        q, k, v, context, sums = saved[s]
        g_out = dot(ga_low, context, (0, 0))
        g_context = by_head(dot(ga_low, a_blocks[s][:, 3 * part :], (1, 0)).astype(bf16))
        gq, gk, gv = attend_backward(q, k, v, g_context, sums, same_doc)
        gq, gk, gv = (by_rows(gq), by_rows(gk), by_rows(gv))
        g_bq.append(jnp.sum(gq.astype(f32), 0))
        g_bv.append(jnp.sum(gv.astype(f32), 0))
        g_qkv = jnp.concatenate([gq, gk, gv], axis=1)
        g_tokens = g_tokens + dot(g_qkv, a_blocks[s][:, : 3 * part], (1, 1))
        g_mixed.append(jnp.concatenate([dot(tokens, g_qkv, (0, 0)), g_out], axis=1))
    piece_a = links.reduce(g_mixed)
    pieces = jnp.concatenate([piece_a, piece_u, piece_d]).astype(bf16)
    step = width // CUBE
    whole = links.ordered(links.spread(pieces)).reshape(CUBE, 3, step, width)
    whole = whole.transpose(1, 0, 2, 3).reshape(3, width, width).astype(f32)
    g_a, g_u, g_d = (whole[0], whole[1], whole[2])
    shared = jnp.stack([g_gain1, g_bias1, g_b_out, g_gain2, g_bias2, g_b_down])
    shared = lax.psum(shared, ("dp", "mp"))
    split = [jnp.concatenate([g_bq[s], g_bv[s], g_b_up[s]]) for s in slots]
    mine = split[0] + sum((links.shift(split[s], -s) for s in range(1, mp)))
    mine = lax.psum(mine, "dp")
    return (
        out_tokens.astype(bf16),
        g_tokens.astype(bf16),
        g_a[:, :part],
        mine[:part],
        g_a[:, part : 2 * part],
        g_a[:, 2 * part : 3 * part],
        mine[part : 2 * part],
        g_a[:, 3 * part :].T,
        shared[2],
        shared[0],
        shared[1],
        g_u,
        mine[2 * part :],
        g_d,
        shared[5],
        shared[3],
        shared[4],
    )


def solution(mesh):
    rows, cols = (P(("dp", "mp"), None), P(None, "mp"))
    in_specs = (
        rows,
        P("dp", None),
        cols,
        P("mp"),
        cols,
        cols,
        P("mp"),
        P("mp", None),
        P(),
        P(),
        P(),
        cols,
        P("mp"),
        P("mp", None),
        P(),
        P(),
        P(),
        rows,
    )
    out_specs = (
        rows,
        rows,
        cols,
        P("mp"),
        cols,
        cols,
        P("mp"),
        P("mp", None),
        P(),
        P(),
        P(),
        cols,
        P("mp"),
        P("mp", None),
        P(),
        P(),
        P(),
    )
    dp, mp = (mesh.shape["dp"], mesh.shape["mp"])

    def step(*args):
        return per_device(dp, mp, *args)

    return jax.shard_map(step, mesh=mesh, in_specs=in_specs, out_specs=out_specs, check_vma=False)
```

profile of v0, /device:TPU:0, one launch (start us, length us, event | category | flops | bytes accessed | tf_op | source)
XLA Modules:
  0.0 417.6 jit_solution(2598088407525156642)
XLA Ops:
  2.4 3.0 collective-permute-start.25
  5.5 2.6 collective-permute-start.26
  9.4 2.1 concatenate.93
  31.6 3.6 collective-permute-done.11
  39.1 3.0 collective-permute-start.15
  44.5 3.0 collective-permute-done.14
  51.8 4.2 %collective-permute-done.15 = bf16[96,768]{1,0:T(8,128)(2,1)S(1)} collective-permute-done((bf16[96,768]{1,0:T(8,128)(2,1)S(1)}, bf16[96,768]{1,0:T(8,128)(2,1)S(1)}, u32[]{:S(2)}, u32[]{:S(2)}) %collective-permute-start.15) | collective-permute-done | bytes 147488 | tf_op jit(solution)/shard_map/ppermute | solution.py:53
  59.2 2.6 collective-permute-done.29
  63.4 6.3 %collective-permute-done.4 = bf16[288,768]{1,0:T(8,128)(2,1)S(1)} collective-permute-done((bf16[288,768]{1,0:T(8,128)(2,1)S(1)}, bf16[288,768]{1,0:T(8,128)(2,1)S(1)}, u32[]{:S(2)}, u32[]{:S(2)}) %collective-permute-start.4) | collective-permute-done | bytes 442400 | tf_op jit(solution)/shard_map/ppermute | solution.py:56
  75.7 7.0 %collective-permute-done.18 = bf16[288,768]{1,0:T(8,128)(2,1)S(1)} collective-permute-done((bf16[288,768]{1,0:T(8,128)(2,1)S(1)}, bf16[288,768]{1,0:T(8,128)(2,1)S(1)}, u32[]{:S(2)}, u32[]{:S(2)}) %collective-permute-start.18) | collective-permute-done | bytes 442400 | tf_op jit(solution)/shard_map/ppermute | solution.py:56
  85.9 3.2 collective-permute-done.33
  89.6 3.7 collective-permute-done.8
  93.4 2.3 collective-permute-done.22
  116.2 2.0 multiply_convert_fusion.7
  126.7 2.1 fusion.177
  178.9 2.0 copy-done.6
  183.6 2.0 copy-done.7
  193.9 2.4 copy.90
  199.2 2.4 copy.89
  204.4 2.4 copy.88
  206.8 2.3 pad_maximum_fusion
  209.3 2.0 copy-done.5
  216.0 3.2 collective-permute-start.68
  225.7 6.5 %collective-permute-start.70 = (f32[1152]{0:T(1024)S(1)}, f32[1152]{0:T(1024)S(1)}, u32[]{:S(2)}, u32[]{:S(2)}) collective-permute-start(f32[1152]{0:T(1024)S(1)} %concatenate.115), channel_id=1, source_target_pairs={{0,1},{1,2},{2,3},{3,0},{4,5},{5,6},{6,7},{7,4},{8,9},{9,10},{10,1... | collective-permute-start | bytes 13832 | tf_op jit(solution)/shard_map/ppermute | solution.py:53
  232.7 40.8 %psum.15 = f32[6,768]{1,0:T(8,128)S(1)} all-reduce(f32[6,768]{1,0:T(8,128)S(1)} %stack.372), channel_id=1, replica_groups=mesh['dp'=8,'mp'=4] {'dp','mp'}, use_global_device_ids=true, to_apply=%region_39.40 | all-reduce | flops 4608 | bytes 36864 | tf_op jit(solution)/shard_map/psum | solution.py:237
  274.2 5.6 %fusion.59 = (bf16[4,96,768]{2,1,0:T(8,128)(2,1)S(1)}, bf16[4,96,768]{2,1,0:T(8,128)(2,1)S(1)}, bf16[4,96,768]{2,1,0:T(8,128)(2,1)S(1)}, bf16[4,96,768]{2,1,0:T(...) fusion(bf16[4,8,96,768]{3,2,0,1:T(8,128)(2,1)} %copy-done.6, ...), kind=kLoop, calls=%fused_computation.155 | loop fusion | flops 9437184 | bytes 14155792 | tf_op jit(solution)/shard_map/convert_element_type | solution.py:96
  280.0 2.3 collective-permute-start.53
  284.8 2.2 fusion.67
  287.3 9.3 %collective-permute-done.53 = bf16[2,2,96,768]{3,2,1,0:T(8,128)(2,1)S(1)} collective-permute-done((bf16[2,2,96,768]{3,2,1,0:T(8,128)(2,1)S(1)}, bf16[2,2,96,768]{3,2,1,0:T(8,128)(2,1)S(1)}, u32[]{:S(2)}, u32[]{:S(2)}) %collective-permute-start.53) | collective-permute-done | bytes 589856 | tf_op jit(solution)/shard_map/ppermute | solution.py:56
  296.5 2.0 collective-permute-start.48
  300.3 8.9 %collective-permute-done.45 = bf16[2,2,96,768]{3,2,1,0:T(8,128)(2,1)S(1)} collective-permute-done((bf16[2,2,96,768]{3,2,1,0:T(8,128)(2,1)S(1)}, bf16[2,2,96,768]{3,2,1,0:T(8,128)(2,1)S(1)}, u32[]{:S(2)}, u32[]{:S(2)}) %collective-permute-start.45) | collective-permute-done | bytes 589856 | tf_op jit(solution)/shard_map/ppermute | solution.py:56
  309.2 2.0 collective-permute-start.40
  311.5 8.7 %collective-permute-done.37 = bf16[2,2,96,768]{3,2,1,0:T(8,128)(2,1)S(1)} collective-permute-done((bf16[2,2,96,768]{3,2,1,0:T(8,128)(2,1)S(1)}, bf16[2,2,96,768]{3,2,1,0:T(8,128)(2,1)S(1)}, u32[]{:S(2)}, u32[]{:S(2)}) %collective-permute-start.37) | collective-permute-done | bytes 589856 | tf_op jit(solution)/shard_map/ppermute | solution.py:56
  322.0 3.5 collective-permute-done.40
  325.5 2.0 collective-permute-start.46
  327.6 4.2 %collective-permute-done.54 = bf16[2,96,768]{2,1,0:T(8,128)(2,1)S(1)} collective-permute-done((bf16[2,96,768]{2,1,0:T(8,128)(2,1)S(1)}, bf16[2,96,768]{2,1,0:T(8,128)(2,1)S(1)}, u32[]{:S(2)}, u32[]{:S(2)}) %collective-permute-start.54) | collective-permute-done | bytes 294944 | tf_op jit(solution)/shard_map/ppermute | solution.py:56
  331.8 2.0 collective-permute-start.49
  335.6 2.0 collective-permute-done.46
  340.7 2.2 collective-permute-start.58
  344.3 2.3 collective-permute-start.55
  347.8 9.6 %collective-permute-done.58 = bf16[96,768]{1,0:T(8,128)(2,1)S(1)} collective-permute-done((bf16[96,768]{1,0:T(8,128)(2,1)S(1)}, bf16[96,768]{1,0:T(8,128)(2,1)S(1)}, u32[]{:S(2)}, u32[]{:S(2)}) %collective-permute-start.58) | collective-permute-done | bytes 147488 | tf_op jit(solution)/shard_map/ppermute | solution.py:53
  358.9 5.4 %collective-permute-start.43 = (bf16[96,768]{1,0:T(8,128)(2,1)S(1)}, bf16[96,768]{1,0:T(8,128)(2,1)S(1)}, u32[]{:S(2)}, u32[]{:S(2)}) collective-permute-start(bf16[96,768]{1,0:T(8,128)(2,1)S(1)} %get-tuple-element.114), channel_id=1, source_target_pairs={{0,1},{1,2},{2,3},{3,0},{4,5},{5,6},{6,7},{7,4},{8,9},{9,10},{10,1... | collective-permute-start | bytes 442376 | tf_op jit(solution)/shard_map/ppermute | solution.py:53
  364.3 4.2 %collective-permute-done.50 = bf16[96,768]{1,0:T(8,128)(2,1)S(1)} collective-permute-done((bf16[96,768]{1,0:T(8,128)(2,1)S(1)}, bf16[96,768]{1,0:T(8,128)(2,1)S(1)}, u32[]{:S(2)}, u32[]{:S(2)}) %collective-permute-start.50) | collective-permute-done | bytes 147488 | tf_op jit(solution)/shard_map/ppermute | solution.py:53
  368.5 3.4 collective-permute-done.47
  372.3 2.5 collective-permute-start.69
  379.2 18.9 %psum.14 = f32[1152]{0:T(1024)S(1)} all-reduce(f32[1152]{0:T(1024)S(1)} %add_add_fusion.3), channel_id=1, replica_groups=mesh['dp'=8,'mp'=4] {'dp'}, use_global_device_ids=true, to_apply=%region_32.33 | all-reduce | flops 1152 | bytes 9216 | tf_op jit(solution)/shard_map/psum | solution.py:240
  400.5 4.9 %collective-permute-done.65 = bf16[144,768]{1,0:T(8,128)(2,1)S(1)} collective-permute-done((bf16[144,768]{1,0:T(8,128)(2,1)S(1)}, bf16[144,768]{1,0:T(8,128)(2,1)S(1)}, u32[]{:S(2)}, u32[]{:S(2)}) %collective-permute-start.65) | collective-permute-done | bytes 221216 | tf_op jit(solution)/shard_map/ppermute | solution.py:56
  409.9 2.7 fusion.180
  (561 shorter events, 186.7 us)
Async XLA Ops:
  2.4 32.8 %collective-permute-start.25 = (bf16[96,768]{1,0:T(8,128)(2,1)}, bf16[96,768]{1,0:T(8,128)(2,1)}, u32[]{:S(2)}, u32[]{:S(2)}) collective-permute-start(bf16[96,768]{1,0:T(8,128)(2,1)} %constant_dynamic-slice_fusion), channel_id=1, source_target_pairs={{0,1},{1,2},{2,3},{3,0},{4,5},{5,6},{6,7},{7,4},{8,9},{9,10},{10,1... | collective-permute-start | bytes 442376 | tf_op jit(solution)/shard_map/ppermute | solution.py:53
  5.5 31.1 %collective-permute-start.26 = (bf16[96,768]{1,0:T(8,128)(2,1)}, bf16[96,768]{1,0:T(8,128)(2,1)}, u32[]{:S(2)}, u32[]{:S(2)}) collective-permute-start(bf16[96,768]{1,0:T(8,128)(2,1)} %constant_dynamic-slice_fusion), channel_id=1, source_target_pairs={{0,2},{1,3},{2,0},{3,1},{4,6},{5,7},{6,4},{7,5},{8,10},{9,11},{10,... | collective-permute-start | bytes 442376 | tf_op jit(solution)/shard_map/ppermute | solution.py:53
  8.1 31.1 %collective-permute-start.27 = (bf16[96,768]{1,0:T(8,128)(2,1)}, bf16[96,768]{1,0:T(8,128)(2,1)}, u32[]{:S(2)}, u32[]{:S(2)}) collective-permute-start(bf16[96,768]{1,0:T(8,128)(2,1)} %constant_dynamic-slice_fusion), channel_id=1, source_target_pairs={{0,3},{1,0},{2,1},{3,2},{4,7},{5,4},{6,5},{7,6},{8,11},{9,8},{10,9... | collective-permute-start | bytes 442376 | tf_op jit(solution)/shard_map/ppermute | solution.py:53
  11.5 18.0 %collective-permute-start.13 = (bf16[1152]{0:T(1024)(128)(2,1)S(1)}, bf16[1152]{0:T(1024)(128)(2,1)S(1)}, u32[]{:S(2)}, u32[]{:S(2)}) collective-permute-start(bf16[1152]{0:T(1024)(128)(2,1)S(1)} %concatenate.93), channel_id=1, source_target_pairs={{0,3},{1,0},{2,1},{3,2},{4,7},{5,4},{6,5},{7,6},{8,11},{9,8},{10,9... | collective-permute-start | bytes 6920 | tf_op jit(solution)/shard_map/ppermute | solution.py:53
  11.9 17.8 %collective-permute-start.12 = (bf16[1152]{0:T(1024)(128)(2,1)S(1)}, bf16[1152]{0:T(1024)(128)(2,1)S(1)}, u32[]{:S(2)}, u32[]{:S(2)}) collective-permute-start(bf16[1152]{0:T(1024)(128)(2,1)S(1)} %concatenate.93), channel_id=1, source_target_pairs={{0,2},{1,3},{2,0},{3,1},{4,6},{5,7},{6,4},{7,5},{8,10},{9,11},{10,... | collective-permute-start | bytes 6920 | tf_op jit(solution)/shard_map/ppermute | solution.py:53
  29.7 13.4 %collective-permute-start = (bf16[96,768]{1,0:T(8,128)(2,1)S(1)}, bf16[96,768]{1,0:T(8,128)(2,1)S(1)}, u32[]{:S(2)}, u32[]{:S(2)}) collective-permute-start(bf16[96,768]{1,0:T(8,128)(2,1)S(1)} %fusion.167), channel_id=1, source_target_pairs={{0,1},{1,2},{2,3},{3,0},{4,5},{5,6},{6,7},{7,4},{8,9},{9,10},{10,1... | collective-permute-start | bytes 442376 | tf_op jit(solution)/shard_map/ppermute | solution.py:53
  35.1 13.5 %collective-permute-start.1 = (bf16[96,768]{1,0:T(8,128)(2,1)S(1)}, bf16[96,768]{1,0:T(8,128)(2,1)S(1)}, u32[]{:S(2)}, u32[]{:S(2)}) collective-permute-start(bf16[96,768]{1,0:T(8,128)(2,1)S(1)} %fusion.167), channel_id=1, source_target_pairs={{0,2},{1,3},{2,0},{3,1},{4,6},{5,7},{6,4},{7,5},{8,10},{9,11},{10,... | collective-permute-start | bytes 442376 | tf_op jit(solution)/shard_map/ppermute | solution.py:53
  35.2 15.0 %collective-permute-start.2 = (bf16[96,768]{1,0:T(8,128)(2,1)S(1)}, bf16[96,768]{1,0:T(8,128)(2,1)S(1)}, u32[]{:S(2)}, u32[]{:S(2)}) collective-permute-start(bf16[96,768]{1,0:T(8,128)(2,1)S(1)} %fusion.167), channel_id=1, source_target_pairs={{0,3},{1,0},{2,1},{3,2},{4,7},{5,4},{6,5},{7,6},{8,11},{9,8},{10,9... | collective-permute-start | bytes 442376 | tf_op jit(solution)/shard_map/ppermute | solution.py:53
  36.6 10.9 %collective-permute-start.14 = (bf16[96,768]{1,0:T(8,128)(2,1)S(1)}, bf16[96,768]{1,0:T(8,128)(2,1)S(1)}, u32[]{:S(2)}, u32[]{:S(2)}) collective-permute-start(bf16[96,768]{1,0:T(8,128)(2,1)S(1)} %constant_dynamic-slice_fusion.1), channel_id=1, source_target_pairs={{0,1},{1,2},{2,3},{3,0},{4,5},{5,6},{6,7},{7,4},{8,9},{9,10},{10,1... | collective-permute-start | bytes 442376 | tf_op jit(solution)/shard_map/ppermute | solution.py:53
  39.1 16.8 %collective-permute-start.15 = (bf16[96,768]{1,0:T(8,128)(2,1)S(1)}, bf16[96,768]{1,0:T(8,128)(2,1)S(1)}, u32[]{:S(2)}, u32[]{:S(2)}) collective-permute-start(bf16[96,768]{1,0:T(8,128)(2,1)S(1)} %constant_dynamic-slice_fusion.1), channel_id=1, source_target_pairs={{0,2},{1,3},{2,0},{3,1},{4,6},{5,7},{6,4},{7,5},{8,10},{9,11},{10,... | collective-permute-start | bytes 442376 | tf_op jit(solution)/shard_map/ppermute | solution.py:53
  43.1 14.4 %collective-permute-start.16 = (bf16[96,768]{1,0:T(8,128)(2,1)S(1)}, bf16[96,768]{1,0:T(8,128)(2,1)S(1)}, u32[]{:S(2)}, u32[]{:S(2)}) collective-permute-start(bf16[96,768]{1,0:T(8,128)(2,1)S(1)} %constant_dynamic-slice_fusion.1), channel_id=1, source_target_pairs={{0,3},{1,0},{2,1},{3,2},{4,7},{5,4},{6,5},{7,6},{8,11},{9,8},{10,9... | collective-permute-start | bytes 442376 | tf_op jit(solution)/shard_map/ppermute | solution.py:53
  47.5 25.3 %collective-permute-start.28 = (bf16[288,768]{1,0:T(8,128)(2,1)S(1)}, bf16[288,768]{1,0:T(8,128)(2,1)S(1)}, u32[]{:S(2)}, u32[]{:S(2)}) collective-permute-start(bf16[288,768]{1,0:T(8,128)(2,1)S(1)} %constant_dynamic-update-slice_fusion.13), channel_id=1, source_target_pairs={{0,4},{4,0},{8,12},{12,8},{16,20},{20,16},{24,28},{28,24},{1,5},{5... | collective-permute-start | bytes 1327112 | tf_op jit(solution)/shard_map/ppermute | solution.py:56
  48.7 13.1 %collective-permute-start.29 = (bf16[288,768]{1,0:T(8,128)(2,1)S(1)}, bf16[288,768]{1,0:T(8,128)(2,1)S(1)}, u32[]{:S(2)}, u32[]{:S(2)}) collective-permute-start(bf16[288,768]{1,0:T(8,128)(2,1)S(1)} %constant_dynamic-update-slice_fusion.13), channel_id=1, source_target_pairs={{0,8},{4,12},{8,0},{12,4},{16,24},{20,28},{24,16},{28,20},{1,9},{5... | collective-permute-start | bytes 1327112 | tf_op jit(solution)/shard_map/ppermute | solution.py:56
  50.2 13.2 %collective-permute-start.31 = (bf16[288,768]{1,0:T(8,128)(2,1)S(1)}, bf16[288,768]{1,0:T(8,128)(2,1)S(1)}, u32[]{:S(2)}, u32[]{:S(2)}) collective-permute-start(bf16[288,768]{1,0:T(8,128)(2,1)S(1)} %constant_dynamic-update-slice_fusion.13), channel_id=1, source_target_pairs={{0,16},{4,20},{8,24},{12,28},{16,0},{20,4},{24,8},{28,12},{1,17},{... | collective-permute-start | bytes 1327112 | tf_op jit(solution)/shard_map/ppermute | solution.py:56
  56.0 13.7 %collective-permute-start.4 = (bf16[288,768]{1,0:T(8,128)(2,1)S(1)}, bf16[288,768]{1,0:T(8,128)(2,1)S(1)}, u32[]{:S(2)}, u32[]{:S(2)}) collective-permute-start(bf16[288,768]{1,0:T(8,128)(2,1)S(1)} %constant_dynamic-update-slice_fusion.3), channel_id=1, source_target_pairs={{0,8},{4,12},{8,0},{12,4},{16,24},{20,28},{24,16},{28,20},{1,9},{5... | collective-permute-start | bytes 1327112 | tf_op jit(solution)/shard_map/ppermute | solution.py:56
  57.5 13.7 %collective-permute-start.6 = (bf16[288,768]{1,0:T(8,128)(2,1)S(1)}, bf16[288,768]{1,0:T(8,128)(2,1)S(1)}, u32[]{:S(2)}, u32[]{:S(2)}) collective-permute-start(bf16[288,768]{1,0:T(8,128)(2,1)S(1)} %constant_dynamic-update-slice_fusion.3), channel_id=1, source_target_pairs={{0,16},{4,20},{8,24},{12,28},{16,0},{20,4},{24,8},{28,12},{1,17},{... | collective-permute-start | bytes 1327112 | tf_op jit(solution)/shard_map/ppermute | solution.py:56
  61.8 11.7 %collective-permute-start.3 = (bf16[288,768]{1,0:T(8,128)(2,1)S(1)}, bf16[288,768]{1,0:T(8,128)(2,1)S(1)}, u32[]{:S(2)}, u32[]{:S(2)}) collective-permute-start(bf16[288,768]{1,0:T(8,128)(2,1)S(1)} %constant_dynamic-update-slice_fusion.3), channel_id=1, source_target_pairs={{0,4},{4,0},{8,12},{12,8},{16,20},{20,16},{24,28},{28,24},{1,5},{5... | collective-permute-start | bytes 1327112 | tf_op jit(solution)/shard_map/ppermute | solution.py:56
  69.7 13.1 %collective-permute-start.18 = (bf16[288,768]{1,0:T(8,128)(2,1)S(1)}, bf16[288,768]{1,0:T(8,128)(2,1)S(1)}, u32[]{:S(2)}, u32[]{:S(2)}) collective-permute-start(bf16[288,768]{1,0:T(8,128)(2,1)S(1)} %constant_dynamic-update-slice_fusion.8), channel_id=1, source_target_pairs={{0,8},{4,12},{8,0},{12,4},{16,24},{20,28},{24,16},{28,20},{1,9},{5... | collective-permute-start | bytes 1327112 | tf_op jit(solution)/shard_map/ppermute | solution.py:56
  71.2 13.2 %collective-permute-start.20 = (bf16[288,768]{1,0:T(8,128)(2,1)S(1)}, bf16[288,768]{1,0:T(8,128)(2,1)S(1)}, u32[]{:S(2)}, u32[]{:S(2)}) collective-permute-start(bf16[288,768]{1,0:T(8,128)(2,1)S(1)} %constant_dynamic-update-slice_fusion.8), channel_id=1, source_target_pairs={{0,16},{4,20},{8,24},{12,28},{16,0},{20,4},{24,8},{28,12},{1,17},{... | collective-permute-start | bytes 1327112 | tf_op jit(solution)/shard_map/ppermute | solution.py:56
  72.8 16.3 %collective-permute-start.33 = (bf16[144,768]{1,0:T(8,128)(2,1)S(1)}, bf16[144,768]{1,0:T(8,128)(2,1)S(1)}, u32[]{:S(2)}, u32[]{:S(2)}) collective-permute-start(bf16[144,768]{1,0:T(8,128)(2,1)S(1)} %slice.538), channel_id=1, source_target_pairs={{0,16},{4,20},{8,24},{12,28},{16,0},{20,4},{24,8},{28,12},{1,17},{... | collective-permute-start | bytes 663560 | tf_op jit(solution)/shard_map/ppermute | solution.py:56
  73.4 22.3 %collective-permute-start.34 = (bf16[144,768]{1,0:T(8,128)(2,1)S(1)}, bf16[144,768]{1,0:T(8,128)(2,1)S(1)}, u32[]{:S(2)}, u32[]{:S(2)}) collective-permute-start(bf16[144,768]{1,0:T(8,128)(2,1)S(1)} %slice.539), channel_id=1, source_target_pairs={{0,8},{4,12},{8,0},{12,4},{16,24},{20,28},{24,16},{28,20},{1,9},{5... | collective-permute-start | bytes 663560 | tf_op jit(solution)/shard_map/ppermute | solution.py:56
  74.1 19.3 %collective-permute-start.8 = (bf16[144,768]{1,0:T(8,128)(2,1)S(1)}, bf16[144,768]{1,0:T(8,128)(2,1)S(1)}, u32[]{:S(2)}, u32[]{:S(2)}) collective-permute-start(bf16[144,768]{1,0:T(8,128)(2,1)S(1)} %slice.508), channel_id=1, source_target_pairs={{0,16},{4,20},{8,24},{12,28},{16,0},{20,4},{24,8},{28,12},{1,17},{... | collective-permute-start | bytes 663560 | tf_op jit(solution)/shard_map/ppermute | solution.py:56
  82.8 13.6 %collective-permute-start.9 = (bf16[144,768]{1,0:T(8,128)(2,1)S(1)}, bf16[144,768]{1,0:T(8,128)(2,1)S(1)}, u32[]{:S(2)}, u32[]{:S(2)}) collective-permute-start(bf16[144,768]{1,0:T(8,128)(2,1)S(1)} %slice.509), channel_id=1, source_target_pairs={{0,8},{4,12},{8,0},{12,4},{16,24},{20,28},{24,16},{28,20},{1,9},{5... | collective-permute-start | bytes 663560 | tf_op jit(solution)/shard_map/ppermute | solution.py:56
  84.3 11.4 %collective-permute-start.22 = (bf16[144,768]{1,0:T(8,128)(2,1)S(1)}, bf16[144,768]{1,0:T(8,128)(2,1)S(1)}, u32[]{:S(2)}, u32[]{:S(2)}) collective-permute-start(bf16[144,768]{1,0:T(8,128)(2,1)S(1)} %slice.534), channel_id=1, source_target_pairs={{0,16},{4,20},{8,24},{12,28},{16,0},{20,4},{24,8},{28,12},{1,17},{... | collective-permute-start | bytes 663560 | tf_op jit(solution)/shard_map/ppermute | solution.py:56
  98.8 15.6 %collective-permute-start.24 = (bf16[288,768]{1,0:T(8,128)(2,1)S(1)}, bf16[288,768]{1,0:T(8,128)(2,1)S(1)}, u32[]{:S(2)}, u32[]{:S(2)}) collective-permute-start(bf16[288,768]{1,0:T(8,128)(2,1)S(1)} %constant_dynamic-update-slice_fusion.11), channel_id=1, source_target_pairs={{0,4},{4,0},{8,12},{12,8},{16,20},{20,16},{24,28},{28,24},{1,5},{5... | collective-permute-start | bytes 1327112 | tf_op jit(solution)/shard_map/ppermute | solution.py:56
  182.6 91.6 %collective-permute-start.52 = (bf16[4,4,96,768]{3,2,1,0:T(8,128)(2,1)}, bf16[4,4,96,768]{3,2,1,0:T(8,128)(2,1)}, u32[]{:S(2)}, u32[]{:S(2)}) collective-permute-start(bf16[4,4,96,768]{3,2,1,0:T(8,128)(2,1)} %pad_maximum_fusion.9), channel_id=1, source_target_pairs={{0,4},{4,0},{8,12},{12,8},{16,20},{20,16},{24,28},{28,24},{1,5},{5... | collective-permute-start | bytes 7077896 | tf_op jit(solution)/shard_map/ppermute | solution.py:56
  187.2 87.0 %collective-permute-start.44 = (bf16[4,4,96,768]{3,2,1,0:T(8,128)(2,1)}, bf16[4,4,96,768]{3,2,1,0:T(8,128)(2,1)}, u32[]{:S(2)}, u32[]{:S(2)}) collective-permute-start(bf16[4,4,96,768]{3,2,1,0:T(8,128)(2,1)} %pad_maximum_fusion.8), channel_id=1, source_target_pairs={{0,4},{4,0},{8,12},{12,8},{16,20},{20,16},{24,28},{28,24},{1,5},{5... | collective-permute-start | bytes 7077896 | tf_op jit(solution)/shard_map/ppermute | solution.py:56
  213.0 71.2 %collective-permute-start.36 = (bf16[4,4,96,768]{3,2,1,0:T(8,128)(2,1)}, bf16[4,4,96,768]{3,2,1,0:T(8,128)(2,1)}, u32[]{:S(2)}, u32[]{:S(2)}) collective-permute-start(bf16[4,4,96,768]{3,2,1,0:T(8,128)(2,1)} %pad_maximum_fusion.7), channel_id=1, source_target_pairs={{0,4},{4,0},{8,12},{12,8},{16,20},{20,16},{24,28},{28,24},{1,5},{5... | collective-permute-start | bytes 7077896 | tf_op jit(solution)/shard_map/ppermute | solution.py:56
  216.0 162.5 %collective-permute-start.68 = (f32[1152]{0:T(1024)}, f32[1152]{0:T(1024)}, u32[]{:S(2)}, u32[]{:S(2)}) collective-permute-start(f32[1152]{0:T(1024)} %concatenate.113), channel_id=1, source_target_pairs={{0,3},{1,0},{2,1},{3,2},{4,7},{5,4},{6,5},{7,6},{8,11},{9,8},{10,9... | collective-permute-start | bytes 13832 | tf_op jit(solution)/shard_map/ppermute | solution.py:53
  225.7 152.3 %collective-permute-start.70 = (f32[1152]{0:T(1024)S(1)}, f32[1152]{0:T(1024)S(1)}, u32[]{:S(2)}, u32[]{:S(2)}) collective-permute-start(f32[1152]{0:T(1024)S(1)} %concatenate.115), channel_id=1, source_target_pairs={{0,1},{1,2},{2,3},{3,0},{4,5},{5,6},{6,7},{7,4},{8,9},{9,10},{10,1... | collective-permute-start | bytes 13832 | tf_op jit(solution)/shard_map/ppermute | solution.py:53
  280.0 16.6 %collective-permute-start.53 = (bf16[2,2,96,768]{3,2,1,0:T(8,128)(2,1)S(1)}, bf16[2,2,96,768]{3,2,1,0:T(8,128)(2,1)S(1)}, u32[]{:S(2)}, u32[]{:S(2)}) collective-permute-start(bf16[2,2,96,768]{3,2,1,0:T(8,128)(2,1)S(1)} %pad_maximum_fusion.18), channel_id=1, source_target_pairs={{0,8},{4,12},{8,0},{12,4},{16,24},{20,28},{24,16},{28,20},{1,9},{5... | collective-permute-start | bytes 1769480 | tf_op jit(solution)/shard_map/ppermute | solution.py:56
  282.4 16.3 %collective-permute-start.56 = (bf16[2,2,96,768]{3,2,1,0:T(8,128)(2,1)S(1)}, bf16[2,2,96,768]{3,2,1,0:T(8,128)(2,1)S(1)}, u32[]{:S(2)}, u32[]{:S(2)}) collective-permute-start(bf16[2,2,96,768]{3,2,1,0:T(8,128)(2,1)S(1)} %pad_maximum_fusion.19), channel_id=1, source_target_pairs={{0,16},{4,20},{8,24},{12,28},{16,0},{20,4},{24,8},{28,12},{1,17},{... | collective-permute-start | bytes 1769480 | tf_op jit(solution)/shard_map/ppermute | solution.py:56
  284.2 25.0 %collective-permute-start.45 = (bf16[2,2,96,768]{3,2,1,0:T(8,128)(2,1)S(1)}, bf16[2,2,96,768]{3,2,1,0:T(8,128)(2,1)S(1)}, u32[]{:S(2)}, u32[]{:S(2)}) collective-permute-start(bf16[2,2,96,768]{3,2,1,0:T(8,128)(2,1)S(1)} %pad_maximum_fusion.16), channel_id=1, source_target_pairs={{0,8},{4,12},{8,0},{12,4},{16,24},{20,28},{24,16},{28,20},{1,9},{5... | collective-permute-start | bytes 1769480 | tf_op jit(solution)/shard_map/ppermute | solution.py:56
  296.5 14.8 %collective-permute-start.48 = (bf16[2,2,96,768]{3,2,1,0:T(8,128)(2,1)S(1)}, bf16[2,2,96,768]{3,2,1,0:T(8,128)(2,1)S(1)}, u32[]{:S(2)}, u32[]{:S(2)}) collective-permute-start(bf16[2,2,96,768]{3,2,1,0:T(8,128)(2,1)S(1)} %pad_maximum_fusion.17), channel_id=1, source_target_pairs={{0,16},{4,20},{8,24},{12,28},{16,0},{20,4},{24,8},{28,12},{1,17},{... | collective-permute-start | bytes 1769480 | tf_op jit(solution)/shard_map/ppermute | solution.py:56
  298.7 21.5 %collective-permute-start.37 = (bf16[2,2,96,768]{3,2,1,0:T(8,128)(2,1)S(1)}, bf16[2,2,96,768]{3,2,1,0:T(8,128)(2,1)S(1)}, u32[]{:S(2)}, u32[]{:S(2)}) collective-permute-start(bf16[2,2,96,768]{3,2,1,0:T(8,128)(2,1)S(1)} %pad_maximum_fusion.14), channel_id=1, source_target_pairs={{0,8},{4,12},{8,0},{12,4},{16,24},{20,28},{24,16},{28,20},{1,9},{5... | collective-permute-start | bytes 1769480 | tf_op jit(solution)/shard_map/ppermute | solution.py:56
  309.2 16.3 %collective-permute-start.40 = (bf16[2,2,96,768]{3,2,1,0:T(8,128)(2,1)S(1)}, bf16[2,2,96,768]{3,2,1,0:T(8,128)(2,1)S(1)}, u32[]{:S(2)}, u32[]{:S(2)}) collective-permute-start(bf16[2,2,96,768]{3,2,1,0:T(8,128)(2,1)S(1)} %pad_maximum_fusion.15), channel_id=1, source_target_pairs={{0,16},{4,20},{8,24},{12,28},{16,0},{20,4},{24,8},{28,12},{1,17},{... | collective-permute-start | bytes 1769480 | tf_op jit(solution)/shard_map/ppermute | solution.py:56
  311.3 20.5 %collective-permute-start.54 = (bf16[2,96,768]{2,1,0:T(8,128)(2,1)S(1)}, bf16[2,96,768]{2,1,0:T(8,128)(2,1)S(1)}, u32[]{:S(2)}, u32[]{:S(2)}) collective-permute-start(bf16[2,96,768]{2,1,0:T(8,128)(2,1)S(1)} %fusion.127), channel_id=1, source_target_pairs={{0,16},{4,20},{8,24},{12,28},{16,0},{20,4},{24,8},{28,12},{1,17},{... | collective-permute-start | bytes 884744 | tf_op jit(solution)/shard_map/ppermute | solution.py:56
  320.1 13.7 %collective-permute-start.57 = (bf16[2,96,768]{2,1,0:T(8,128)(2,1)S(1)}, bf16[2,96,768]{2,1,0:T(8,128)(2,1)S(1)}, u32[]{:S(2)}, u32[]{:S(2)}) collective-permute-start(bf16[2,96,768]{2,1,0:T(8,128)(2,1)S(1)} %fusion.126), channel_id=1, source_target_pairs={{0,8},{4,12},{8,0},{12,4},{16,24},{20,28},{24,16},{28,20},{1,9},{5... | collective-permute-start | bytes 884744 | tf_op jit(solution)/shard_map/ppermute | solution.py:56
  325.5 12.1 %collective-permute-start.46 = (bf16[2,96,768]{2,1,0:T(8,128)(2,1)S(1)}, bf16[2,96,768]{2,1,0:T(8,128)(2,1)S(1)}, u32[]{:S(2)}, u32[]{:S(2)}) collective-permute-start(bf16[2,96,768]{2,1,0:T(8,128)(2,1)S(1)} %fusion.132), channel_id=1, source_target_pairs={{0,16},{4,20},{8,24},{12,28},{16,0},{20,4},{24,8},{28,12},{1,17},{... | collective-permute-start | bytes 884744 | tf_op jit(solution)/shard_map/ppermute | solution.py:56
  340.7 16.7 %collective-permute-start.58 = (bf16[96,768]{1,0:T(8,128)(2,1)S(1)}, bf16[96,768]{1,0:T(8,128)(2,1)S(1)}, u32[]{:S(2)}, u32[]{:S(2)}) collective-permute-start(bf16[96,768]{1,0:T(8,128)(2,1)S(1)} %get-tuple-element.117), channel_id=1, source_target_pairs={{0,2},{1,3},{2,0},{3,1},{4,6},{5,7},{6,4},{7,5},{8,10},{9,11},{10,... | collective-permute-start | bytes 442376 | tf_op jit(solution)/shard_map/ppermute | solution.py:53
  344.3 13.1 %collective-permute-start.55 = (bf16[96,768]{1,0:T(8,128)(2,1)S(1)}, bf16[96,768]{1,0:T(8,128)(2,1)S(1)}, u32[]{:S(2)}, u32[]{:S(2)}) collective-permute-start(bf16[96,768]{1,0:T(8,128)(2,1)S(1)} %slice_bitcast_fusion.39), channel_id=1, source_target_pairs={{0,3},{1,0},{2,1},{3,2},{4,7},{5,4},{6,5},{7,6},{8,11},{9,8},{10,9... | collective-permute-start | bytes 442376 | tf_op jit(solution)/shard_map/ppermute | solution.py:53
  347.8 11.2 %collective-permute-start.51 = (bf16[96,768]{1,0:T(8,128)(2,1)S(1)}, bf16[96,768]{1,0:T(8,128)(2,1)S(1)}, u32[]{:S(2)}, u32[]{:S(2)}) collective-permute-start(bf16[96,768]{1,0:T(8,128)(2,1)S(1)} %get-tuple-element.116), channel_id=1, source_target_pairs={{0,1},{1,2},{2,3},{3,0},{4,5},{5,6},{6,7},{7,4},{8,9},{9,10},{10,1... | collective-permute-start | bytes 442376 | tf_op jit(solution)/shard_map/ppermute | solution.py:53
  357.4 11.1 %collective-permute-start.50 = (bf16[96,768]{1,0:T(8,128)(2,1)S(1)}, bf16[96,768]{1,0:T(8,128)(2,1)S(1)}, u32[]{:S(2)}, u32[]{:S(2)}) collective-permute-start(bf16[96,768]{1,0:T(8,128)(2,1)S(1)} %get-tuple-element.115), channel_id=1, source_target_pairs={{0,2},{1,3},{2,0},{3,1},{4,6},{5,7},{6,4},{7,5},{8,10},{9,11},{10,... | collective-permute-start | bytes 442376 | tf_op jit(solution)/shard_map/ppermute | solution.py:53
  357.4 14.5 %collective-permute-start.47 = (bf16[96,768]{1,0:T(8,128)(2,1)S(1)}, bf16[96,768]{1,0:T(8,128)(2,1)S(1)}, u32[]{:S(2)}, u32[]{:S(2)}) collective-permute-start(bf16[96,768]{1,0:T(8,128)(2,1)S(1)} %slice_bitcast_fusion.43), channel_id=1, source_target_pairs={{0,3},{1,0},{2,1},{3,2},{4,7},{5,4},{6,5},{7,6},{8,11},{9,8},{10,9... | collective-permute-start | bytes 442376 | tf_op jit(solution)/shard_map/ppermute | solution.py:53
  358.9 13.4 %collective-permute-start.43 = (bf16[96,768]{1,0:T(8,128)(2,1)S(1)}, bf16[96,768]{1,0:T(8,128)(2,1)S(1)}, u32[]{:S(2)}, u32[]{:S(2)}) collective-permute-start(bf16[96,768]{1,0:T(8,128)(2,1)S(1)} %get-tuple-element.114), channel_id=1, source_target_pairs={{0,1},{1,2},{2,3},{3,0},{4,5},{5,6},{6,7},{7,4},{8,9},{9,10},{10,1... | collective-permute-start | bytes 442376 | tf_op jit(solution)/shard_map/ppermute | solution.py:53
  377.8 22.6 %collective-permute-start.60 = (bf16[288,768]{1,0:T(8,128)(2,1)S(1)}, bf16[288,768]{1,0:T(8,128)(2,1)S(1)}, u32[]{:S(2)}, u32[]{:S(2)}) collective-permute-start(bf16[288,768]{1,0:T(8,128)(2,1)S(1)} %pad_maximum_fusion.20), channel_id=1, source_target_pairs={{0,4},{4,0},{8,12},{12,8},{16,20},{20,16},{24,28},{28,24},{1,5},{5... | collective-permute-start | bytes 1327112 | tf_op jit(solution)/shard_map/ppermute | solution.py:56
  377.9 21.5 %collective-permute-start.61 = (bf16[288,768]{1,0:T(8,128)(2,1)S(1)}, bf16[288,768]{1,0:T(8,128)(2,1)S(1)}, u32[]{:S(2)}, u32[]{:S(2)}) collective-permute-start(bf16[288,768]{1,0:T(8,128)(2,1)S(1)} %pad_maximum_fusion.20), channel_id=1, source_target_pairs={{0,8},{4,12},{8,0},{12,4},{16,24},{20,28},{24,16},{28,20},{1,9},{5... | collective-permute-start | bytes 1327112 | tf_op jit(solution)/shard_map/ppermute | solution.py:56
  378.0 21.7 %collective-permute-start.63 = (bf16[288,768]{1,0:T(8,128)(2,1)S(1)}, bf16[288,768]{1,0:T(8,128)(2,1)S(1)}, u32[]{:S(2)}, u32[]{:S(2)}) collective-permute-start(bf16[288,768]{1,0:T(8,128)(2,1)S(1)} %pad_maximum_fusion.20), channel_id=1, source_target_pairs={{0,16},{4,20},{8,24},{12,28},{16,0},{20,4},{24,8},{28,12},{1,17},{... | collective-permute-start | bytes 1327112 | tf_op jit(solution)/shard_map/ppermute | solution.py:56
  (100 other events, 707.1 us)
where the time goes:
time: 423 us; the launch traced here: 418 us
  waiting for transfers between devices  111 us (26%)
  starting transfers between devices  79.4 us (19%)
  matrix products  74.4 us (18%)
  blocking collectives  59.8 us (14%)
  local copies, waits for them, and re-layouts  53.9 us (13%)
  other arithmetic  36.1 us (9%)
    ppermute x47, waiting for transfers between devices, flip(): return lax.ppermute(x, 'dp', [(i, i ^ bit) for i in range(self.dp)])  77.7 us
    dot_general x48, matrix products, dot(): lax.dot_general(left, right, ((dims[:1], dims[1:]), ((), ())), preferred_...  48.4 us
    ppermute x24, starting transfers between devices, shift(): lax.ppermute(x, 'mp', [(i, (i + by) % self.mp) for i in range(self.mp)])  41.3 us
    psum x1, blocking collectives, per_device(): shared = lax.psum(shared, ('dp', 'mp'))  40.8 us
    ppermute x47, starting transfers between devices, flip(): return lax.ppermute(x, 'dp', [(i, i ^ bit) for i in range(self.dp)])  38.1 us
    ppermute x24, waiting for transfers between devices, shift(): lax.ppermute(x, 'mp', [(i, (i + by) % self.mp) for i in range(self.mp)])  32.9 us
    unnamed x229, local copies, waits for them, and re-layouts  27.9 us
    psum x1, blocking collectives, per_device(): mine = lax.psum(mine, 'dp')  18.9 us
  transfers between devices with their start and end apart: 71, of which 36 were waited for; matrix products, arithmetic and copies ran while one was open for 19% of the time, Pallas kernels for 0%

commit v1 on v0

--- a/solution.py
+++ b/solution.py
@@ -234,7 +234,7 @@
     whole = whole.transpose(1, 0, 2, 3).reshape(3, width, width).astype(f32)
     g_a, g_u, g_d = (whole[0], whole[1], whole[2])
     shared = jnp.stack([g_gain1, g_bias1, g_b_out, g_gain2, g_bias2, g_b_down])
-    shared = lax.psum(shared, ("dp", "mp"))
+    shared = lax.psum(lax.psum(shared, "mp"), "dp")
     split = [jnp.concatenate([g_bq[s], g_bv[s], g_b_up[s]]) for s in slots]
     mine = split[0] + sum((links.shift(split[s], -s) for s in range(1, mp)))
     mine = lax.psum(mine, "dp")

time: 423 us -> 398 us (0.941)
  blocking collectives: 59.8 us -> 40.7 us
  matrix products: 74.4 us -> 67.4 us
    psum x1, blocking collectives: 40.8 us -> 16.5 us  [per_device(): shared = lax.psum(lax.psum(shared, 'mp'), 'dp')]
    ppermute x47, waiting for transfers between devices: 77.7 us -> 89.4 us  [flip(): return lax.ppermute(x, 'dp', [(i, i ^ bit) for i in range(self.dp)])]
    ppermute x24, waiting for transfers between devices: 32.9 us -> 24 us  [shift(): lax.ppermute(x, 'mp', [(i, (i + by) % self.mp) for i in range(self.mp)])]
    ppermute x24, starting transfers between devices: 41.3 us -> 48.2 us  [shift(): lax.ppermute(x, 'mp', [(i, (i + by) % self.mp) for i in range(self.mp)])]
    psum x1, blocking collectives: 18.9 us -> 24.1 us  [per_device(): mine = lax.psum(mine, 'dp')]
    ppermute x47, starting transfers between devices: 38.1 us -> 33.4 us  [flip(): return lax.ppermute(x, 'dp', [(i, i ^ bit) for i in range(self.dp)])]
    unnamed x229 -> x207, local copies, waits for them, and re-layouts: 27.9 us -> 29.1 us
  transfers between devices with their start and end apart: 71 -> 71, of which waited for: 36 -> 33; matrix products, arithmetic and copies ran while one was open for 19% -> 19% of each run, Pallas kernels for 0% -> 0%
where the time goes in v1:
time: 398 us; the launch traced here: 393 us
  waiting for transfers between devices  113 us (28%)
  starting transfers between devices  81.6 us (21%)
  matrix products  67.4 us (17%)
  local copies, waits for them, and re-layouts  52.5 us (13%)
  blocking collectives  40.7 us (10%)
  other arithmetic  34.3 us (9%)
    ppermute x47, waiting for transfers between devices, flip(): return lax.ppermute(x, 'dp', [(i, i ^ bit) for i in range(self.dp)])  89.4 us
    ppermute x24, starting transfers between devices, shift(): lax.ppermute(x, 'mp', [(i, (i + by) % self.mp) for i in range(self.mp)])  48.2 us
    dot_general x48, matrix products, dot(): lax.dot_general(left, right, ((dims[:1], dims[1:]), ((), ())), preferred_...  46.1 us
    ppermute x47, starting transfers between devices, flip(): return lax.ppermute(x, 'dp', [(i, i ^ bit) for i in range(self.dp)])  33.4 us
    unnamed x207, local copies, waits for them, and re-layouts  29.1 us
    psum x1, blocking collectives, per_device(): mine = lax.psum(mine, 'dp')  24.1 us
    ppermute x24, waiting for transfers between devices, shift(): lax.ppermute(x, 'mp', [(i, (i + by) % self.mp) for i in range(self.mp)])  24 us
    psum x1, blocking collectives, per_device(): shared = lax.psum(lax.psum(shared, 'mp'), 'dp')  16.5 us
  transfers between devices with their start and end apart: 71, of which 33 were waited for; matrix products, arithmetic and copies ran while one was open for 19% of the time, Pallas kernels for 0%

profile of v1, /device:TPU:0, one launch (start us, length us, event | category | flops | bytes accessed | tf_op | source)
XLA Modules:
  0.0 393.1 jit_solution(18210828468788632115)
XLA Ops:
  2.4 3.0 collective-permute-start.25
  5.5 2.6 collective-permute-start.26
  9.4 2.1 concatenate.93
  17.5 2.0 copy.72
  31.5 3.6 collective-permute-done.11
  39.1 3.0 collective-permute-start.15
  44.5 3.0 collective-permute-done.14
  51.8 4.2 %collective-permute-done.15 = bf16[96,768]{1,0:T(8,128)(2,1)S(1)} collective-permute-done((bf16[96,768]{1,0:T(8,128)(2,1)S(1)}, bf16[96,768]{1,0:T(8,128)(2,1)S(1)}, u32[]{:S(2)}, u32[]{:S(2)}) %collective-permute-start.15) | collective-permute-done | bytes 147488 | tf_op jit(solution)/shard_map/ppermute | solution.py:53
  59.1 2.6 collective-permute-done.29
  63.3 6.3 %collective-permute-done.4 = bf16[288,768]{1,0:T(8,128)(2,1)S(1)} collective-permute-done((bf16[288,768]{1,0:T(8,128)(2,1)S(1)}, bf16[288,768]{1,0:T(8,128)(2,1)S(1)}, u32[]{:S(2)}, u32[]{:S(2)}) %collective-permute-start.4) | collective-permute-done | bytes 442400 | tf_op jit(solution)/shard_map/ppermute | solution.py:56
  75.7 7.0 %collective-permute-done.18 = bf16[288,768]{1,0:T(8,128)(2,1)S(1)} collective-permute-done((bf16[288,768]{1,0:T(8,128)(2,1)S(1)}, bf16[288,768]{1,0:T(8,128)(2,1)S(1)}, u32[]{:S(2)}, u32[]{:S(2)}) %collective-permute-start.18) | collective-permute-done | bytes 442400 | tf_op jit(solution)/shard_map/ppermute | solution.py:56
  85.9 3.2 collective-permute-done.33
  89.6 3.8 collective-permute-done.8
  93.4 2.3 collective-permute-done.22
  116.2 2.0 multiply_convert_fusion.7
  119.0 1.9 multiply_convert_fusion.5
  171.5 2.0 copy-done.6
  176.2 2.0 copy-done.7
  186.5 2.4 copy.90
  191.7 2.4 copy.89
  197.0 2.4 copy.88
  199.6 9.2 %collective-permute-start.70 = (f32[1152]{0:T(1024)S(1)}, f32[1152]{0:T(1024)S(1)}, u32[]{:S(2)}, u32[]{:S(2)}) collective-permute-start(f32[1152]{0:T(1024)S(1)} %concatenate.115), channel_id=1, source_target_pairs={{0,1},{1,2},{2,3},{3,0},{4,5},{5,6},{6,7},{7,4},{8,9},{9,10},{10,1... | collective-permute-start | bytes 13832 | tf_op jit(solution)/shard_map/ppermute | solution.py:53
  209.3 3.9 %collective-permute-start.69 = (f32[1152]{0:T(1024)S(1)}, f32[1152]{0:T(1024)S(1)}, u32[]{:S(2)}, u32[]{:S(2)}) collective-permute-start(f32[1152]{0:T(1024)S(1)} %concatenate.114), channel_id=1, source_target_pairs={{0,2},{1,3},{2,0},{3,1},{4,6},{5,7},{6,4},{7,5},{8,10},{9,11},{10,... | collective-permute-start | bytes 13832 | tf_op jit(solution)/shard_map/ppermute | solution.py:53
  213.4 2.3 pad_maximum_fusion
  215.9 2.0 copy-done.5
  224.2 1.9 add_convert_fusion
  226.1 16.5 %psum.22 = f32[6,768]{1,0:T(8,128)S(1)} all-reduce(f32[6,768]{1,0:T(8,128)S(1)} %stack.372), channel_id=1, replica_groups=mesh['dp'=8,'mp'=4] {'mp'}, use_global_device_ids=true, to_apply=%region_39.40 | all-reduce | flops 4608 | bytes 36864 | tf_op jit(solution)/shard_map/psum | solution.py:237
  242.9 24.1 %all-reduce = (f32[1152]{0:T(1024)S(1)}, f32[6,768]{1,0:T(8,128)S(1)}) all-reduce(f32[1152]{0:T(1024)S(1)} %add_add_fusion.3, f32[6,768]{1,0:T(8,128)S(1)} %psum.22), channel_id=1, replica_groups=mesh['dp'=8,'mp'=4] {'dp'}, use_global_device_ids=true, to_apply=%region_32.33 | all-reduce | flops 5760 | bytes 46080 | tf_op jit(solution)/shard_map/psum | solution.py:240
  267.7 5.6 %fusion.59 = (bf16[4,96,768]{2,1,0:T(8,128)(2,1)S(1)}, bf16[4,96,768]{2,1,0:T(8,128)(2,1)S(1)}, bf16[4,96,768]{2,1,0:T(8,128)(2,1)S(1)}, bf16[4,96,768]{2,1,0:T(...) fusion(bf16[4,8,96,768]{3,2,0,1:T(8,128)(2,1)} %copy-done.6, ...), kind=kLoop, calls=%fused_computation.155 | loop fusion | flops 9437184 | bytes 14155792 | tf_op jit(solution)/shard_map/convert_element_type | solution.py:96
  274.3 2.1 collective-permute-start.45
  278.1 2.2 fusion.67
  280.7 9.1 %collective-permute-done.53 = bf16[2,2,96,768]{3,2,1,0:T(8,128)(2,1)S(1)} collective-permute-done((bf16[2,2,96,768]{3,2,1,0:T(8,128)(2,1)S(1)}, bf16[2,2,96,768]{3,2,1,0:T(8,128)(2,1)S(1)}, u32[]{:S(2)}, u32[]{:S(2)}) %collective-permute-start.53) | collective-permute-done | bytes 589856 | tf_op jit(solution)/shard_map/ppermute | solution.py:56
  292.0 10.4 %collective-permute-done.45 = bf16[2,2,96,768]{3,2,1,0:T(8,128)(2,1)S(1)} collective-permute-done((bf16[2,2,96,768]{3,2,1,0:T(8,128)(2,1)S(1)}, bf16[2,2,96,768]{3,2,1,0:T(8,128)(2,1)S(1)}, u32[]{:S(2)}, u32[]{:S(2)}) %collective-permute-start.45) | collective-permute-done | bytes 589856 | tf_op jit(solution)/shard_map/ppermute | solution.py:56
  303.2 11.9 %collective-permute-done.37 = bf16[2,2,96,768]{3,2,1,0:T(8,128)(2,1)S(1)} collective-permute-done((bf16[2,2,96,768]{3,2,1,0:T(8,128)(2,1)S(1)}, bf16[2,2,96,768]{3,2,1,0:T(8,128)(2,1)S(1)}, u32[]{:S(2)}, u32[]{:S(2)}) %collective-permute-start.37) | collective-permute-done | bytes 589856 | tf_op jit(solution)/shard_map/ppermute | solution.py:56
  315.8 5.8 %collective-permute-done.54 = bf16[2,96,768]{2,1,0:T(8,128)(2,1)S(1)} collective-permute-done((bf16[2,96,768]{2,1,0:T(8,128)(2,1)S(1)}, bf16[2,96,768]{2,1,0:T(8,128)(2,1)S(1)}, u32[]{:S(2)}, u32[]{:S(2)}) %collective-permute-start.54) | collective-permute-done | bytes 294944 | tf_op jit(solution)/shard_map/ppermute | solution.py:56
  321.6 2.0 collective-permute-start.41
  323.9 4.0 %collective-permute-done.46 = bf16[2,96,768]{2,1,0:T(8,128)(2,1)S(1)} collective-permute-done((bf16[2,96,768]{2,1,0:T(8,128)(2,1)S(1)}, bf16[2,96,768]{2,1,0:T(8,128)(2,1)S(1)}, u32[]{:S(2)}, u32[]{:S(2)}) %collective-permute-start.46) | collective-permute-done | bytes 294944 | tf_op jit(solution)/shard_map/ppermute | solution.py:56
  329.8 2.0 collective-permute-done.38
  333.7 2.2 collective-permute-start.47
  335.9 5.2 %collective-permute-done.58 = bf16[96,768]{1,0:T(8,128)(2,1)S(1)} collective-permute-done((bf16[96,768]{1,0:T(8,128)(2,1)S(1)}, bf16[96,768]{1,0:T(8,128)(2,1)S(1)}, u32[]{:S(2)}, u32[]{:S(2)}) %collective-permute-start.58) | collective-permute-done | bytes 147488 | tf_op jit(solution)/shard_map/ppermute | solution.py:53
  341.8 7.9 %collective-permute-start.42 = (bf16[96,768]{1,0:T(8,128)(2,1)S(1)}, bf16[96,768]{1,0:T(8,128)(2,1)S(1)}, u32[]{:S(2)}, u32[]{:S(2)}) collective-permute-start(bf16[96,768]{1,0:T(8,128)(2,1)S(1)} %get-tuple-element.115), channel_id=1, source_target_pairs={{0,2},{1,3},{2,0},{3,1},{4,6},{5,7},{6,4},{7,5},{8,10},{9,11},{10,... | collective-permute-start | bytes 442376 | tf_op jit(solution)/shard_map/ppermute | solution.py:53
  349.7 3.6 collective-permute-start.39
  353.5 6.8 %collective-permute-done.42 = bf16[96,768]{1,0:T(8,128)(2,1)S(1)} collective-permute-done((bf16[96,768]{1,0:T(8,128)(2,1)S(1)}, bf16[96,768]{1,0:T(8,128)(2,1)S(1)}, u32[]{:S(2)}, u32[]{:S(2)}) %collective-permute-start.42) | collective-permute-done | bytes 147488 | tf_op jit(solution)/shard_map/ppermute | solution.py:53
  360.9 2.1 collective-permute-start.63
  364.3 8.7 %collective-permute-done.61 = bf16[288,768]{1,0:T(8,128)(2,1)S(1)} collective-permute-done((bf16[288,768]{1,0:T(8,128)(2,1)S(1)}, bf16[288,768]{1,0:T(8,128)(2,1)S(1)}, u32[]{:S(2)}, u32[]{:S(2)}) %collective-permute-start.61) | collective-permute-done | bytes 442400 | tf_op jit(solution)/shard_map/ppermute | solution.py:56
  373.1 2.5 collective-permute-start.65
  376.5 4.3 %collective-permute-done.65 = bf16[144,768]{1,0:T(8,128)(2,1)S(1)} collective-permute-done((bf16[144,768]{1,0:T(8,128)(2,1)S(1)}, bf16[144,768]{1,0:T(8,128)(2,1)S(1)}, u32[]{:S(2)}, u32[]{:S(2)}) %collective-permute-start.65) | collective-permute-done | bytes 221216 | tf_op jit(solution)/shard_map/ppermute | solution.py:56
  385.4 2.7 fusion.180
  (539 shorter events, 165.3 us)
Async XLA Ops:
  2.4 32.7 %collective-permute-start.25 = (bf16[96,768]{1,0:T(8,128)(2,1)}, bf16[96,768]{1,0:T(8,128)(2,1)}, u32[]{:S(2)}, u32[]{:S(2)}) collective-permute-start(bf16[96,768]{1,0:T(8,128)(2,1)} %constant_dynamic-slice_fusion), channel_id=1, source_target_pairs={{0,1},{1,2},{2,3},{3,0},{4,5},{5,6},{6,7},{7,4},{8,9},{9,10},{10,1... | collective-permute-start | bytes 442376 | tf_op jit(solution)/shard_map/ppermute | solution.py:53
  5.5 31.1 %collective-permute-start.26 = (bf16[96,768]{1,0:T(8,128)(2,1)}, bf16[96,768]{1,0:T(8,128)(2,1)}, u32[]{:S(2)}, u32[]{:S(2)}) collective-permute-start(bf16[96,768]{1,0:T(8,128)(2,1)} %constant_dynamic-slice_fusion), channel_id=1, source_target_pairs={{0,2},{1,3},{2,0},{3,1},{4,6},{5,7},{6,4},{7,5},{8,10},{9,11},{10,... | collective-permute-start | bytes 442376 | tf_op jit(solution)/shard_map/ppermute | solution.py:53
  8.1 31.1 %collective-permute-start.27 = (bf16[96,768]{1,0:T(8,128)(2,1)}, bf16[96,768]{1,0:T(8,128)(2,1)}, u32[]{:S(2)}, u32[]{:S(2)}) collective-permute-start(bf16[96,768]{1,0:T(8,128)(2,1)} %constant_dynamic-slice_fusion), channel_id=1, source_target_pairs={{0,3},{1,0},{2,1},{3,2},{4,7},{5,4},{6,5},{7,6},{8,11},{9,8},{10,9... | collective-permute-start | bytes 442376 | tf_op jit(solution)/shard_map/ppermute | solution.py:53
  11.5 18.0 %collective-permute-start.13 = (bf16[1152]{0:T(1024)(128)(2,1)S(1)}, bf16[1152]{0:T(1024)(128)(2,1)S(1)}, u32[]{:S(2)}, u32[]{:S(2)}) collective-permute-start(bf16[1152]{0:T(1024)(128)(2,1)S(1)} %concatenate.93), channel_id=1, source_target_pairs={{0,3},{1,0},{2,1},{3,2},{4,7},{5,4},{6,5},{7,6},{8,11},{9,8},{10,9... | collective-permute-start | bytes 6920 | tf_op jit(solution)/shard_map/ppermute | solution.py:53
  11.9 17.7 %collective-permute-start.12 = (bf16[1152]{0:T(1024)(128)(2,1)S(1)}, bf16[1152]{0:T(1024)(128)(2,1)S(1)}, u32[]{:S(2)}, u32[]{:S(2)}) collective-permute-start(bf16[1152]{0:T(1024)(128)(2,1)S(1)} %concatenate.93), channel_id=1, source_target_pairs={{0,2},{1,3},{2,0},{3,1},{4,6},{5,7},{6,4},{7,5},{8,10},{9,11},{10,... | collective-permute-start | bytes 6920 | tf_op jit(solution)/shard_map/ppermute | solution.py:53
  29.7 13.4 %collective-permute-start = (bf16[96,768]{1,0:T(8,128)(2,1)S(1)}, bf16[96,768]{1,0:T(8,128)(2,1)S(1)}, u32[]{:S(2)}, u32[]{:S(2)}) collective-permute-start(bf16[96,768]{1,0:T(8,128)(2,1)S(1)} %fusion.167), channel_id=1, source_target_pairs={{0,1},{1,2},{2,3},{3,0},{4,5},{5,6},{6,7},{7,4},{8,9},{9,10},{10,1... | collective-permute-start | bytes 442376 | tf_op jit(solution)/shard_map/ppermute | solution.py:53
  35.1 13.5 %collective-permute-start.1 = (bf16[96,768]{1,0:T(8,128)(2,1)S(1)}, bf16[96,768]{1,0:T(8,128)(2,1)S(1)}, u32[]{:S(2)}, u32[]{:S(2)}) collective-permute-start(bf16[96,768]{1,0:T(8,128)(2,1)S(1)} %fusion.167), channel_id=1, source_target_pairs={{0,2},{1,3},{2,0},{3,1},{4,6},{5,7},{6,4},{7,5},{8,10},{9,11},{10,... | collective-permute-start | bytes 442376 | tf_op jit(solution)/shard_map/ppermute | solution.py:53
  35.2 15.0 %collective-permute-start.2 = (bf16[96,768]{1,0:T(8,128)(2,1)S(1)}, bf16[96,768]{1,0:T(8,128)(2,1)S(1)}, u32[]{:S(2)}, u32[]{:S(2)}) collective-permute-start(bf16[96,768]{1,0:T(8,128)(2,1)S(1)} %fusion.167), channel_id=1, source_target_pairs={{0,3},{1,0},{2,1},{3,2},{4,7},{5,4},{6,5},{7,6},{8,11},{9,8},{10,9... | collective-permute-start | bytes 442376 | tf_op jit(solution)/shard_map/ppermute | solution.py:53
  39.1 16.8 %collective-permute-start.15 = (bf16[96,768]{1,0:T(8,128)(2,1)S(1)}, bf16[96,768]{1,0:T(8,128)(2,1)S(1)}, u32[]{:S(2)}, u32[]{:S(2)}) collective-permute-start(bf16[96,768]{1,0:T(8,128)(2,1)S(1)} %constant_dynamic-slice_fusion.1), channel_id=1, source_target_pairs={{0,2},{1,3},{2,0},{3,1},{4,6},{5,7},{6,4},{7,5},{8,10},{9,11},{10,... | collective-permute-start | bytes 442376 | tf_op jit(solution)/shard_map/ppermute | solution.py:53
  43.1 14.4 %collective-permute-start.16 = (bf16[96,768]{1,0:T(8,128)(2,1)S(1)}, bf16[96,768]{1,0:T(8,128)(2,1)S(1)}, u32[]{:S(2)}, u32[]{:S(2)}) collective-permute-start(bf16[96,768]{1,0:T(8,128)(2,1)S(1)} %constant_dynamic-slice_fusion.1), channel_id=1, source_target_pairs={{0,3},{1,0},{2,1},{3,2},{4,7},{5,4},{6,5},{7,6},{8,11},{9,8},{10,9... | collective-permute-start | bytes 442376 | tf_op jit(solution)/shard_map/ppermute | solution.py:53
  47.5 25.3 %collective-permute-start.28 = (bf16[288,768]{1,0:T(8,128)(2,1)S(1)}, bf16[288,768]{1,0:T(8,128)(2,1)S(1)}, u32[]{:S(2)}, u32[]{:S(2)}) collective-permute-start(bf16[288,768]{1,0:T(8,128)(2,1)S(1)} %constant_dynamic-update-slice_fusion.13), channel_id=1, source_target_pairs={{0,4},{4,0},{8,12},{12,8},{16,20},{20,16},{24,28},{28,24},{1,5},{5... | collective-permute-start | bytes 1327112 | tf_op jit(solution)/shard_map/ppermute | solution.py:56
  48.6 13.1 %collective-permute-start.29 = (bf16[288,768]{1,0:T(8,128)(2,1)S(1)}, bf16[288,768]{1,0:T(8,128)(2,1)S(1)}, u32[]{:S(2)}, u32[]{:S(2)}) collective-permute-start(bf16[288,768]{1,0:T(8,128)(2,1)S(1)} %constant_dynamic-update-slice_fusion.13), channel_id=1, source_target_pairs={{0,8},{4,12},{8,0},{12,4},{16,24},{20,28},{24,16},{28,20},{1,9},{5... | collective-permute-start | bytes 1327112 | tf_op jit(solution)/shard_map/ppermute | solution.py:56
  50.1 13.2 %collective-permute-start.31 = (bf16[288,768]{1,0:T(8,128)(2,1)S(1)}, bf16[288,768]{1,0:T(8,128)(2,1)S(1)}, u32[]{:S(2)}, u32[]{:S(2)}) collective-permute-start(bf16[288,768]{1,0:T(8,128)(2,1)S(1)} %constant_dynamic-update-slice_fusion.13), channel_id=1, source_target_pairs={{0,16},{4,20},{8,24},{12,28},{16,0},{20,4},{24,8},{28,12},{1,17},{... | collective-permute-start | bytes 1327112 | tf_op jit(solution)/shard_map/ppermute | solution.py:56
  56.0 13.7 %collective-permute-start.4 = (bf16[288,768]{1,0:T(8,128)(2,1)S(1)}, bf16[288,768]{1,0:T(8,128)(2,1)S(1)}, u32[]{:S(2)}, u32[]{:S(2)}) collective-permute-start(bf16[288,768]{1,0:T(8,128)(2,1)S(1)} %constant_dynamic-update-slice_fusion.3), channel_id=1, source_target_pairs={{0,8},{4,12},{8,0},{12,4},{16,24},{20,28},{24,16},{28,20},{1,9},{5... | collective-permute-start | bytes 1327112 | tf_op jit(solution)/shard_map/ppermute | solution.py:56
  57.5 13.7 %collective-permute-start.6 = (bf16[288,768]{1,0:T(8,128)(2,1)S(1)}, bf16[288,768]{1,0:T(8,128)(2,1)S(1)}, u32[]{:S(2)}, u32[]{:S(2)}) collective-permute-start(bf16[288,768]{1,0:T(8,128)(2,1)S(1)} %constant_dynamic-update-slice_fusion.3), channel_id=1, source_target_pairs={{0,16},{4,20},{8,24},{12,28},{16,0},{20,4},{24,8},{28,12},{1,17},{... | collective-permute-start | bytes 1327112 | tf_op jit(solution)/shard_map/ppermute | solution.py:56
  69.6 13.1 %collective-permute-start.18 = (bf16[288,768]{1,0:T(8,128)(2,1)S(1)}, bf16[288,768]{1,0:T(8,128)(2,1)S(1)}, u32[]{:S(2)}, u32[]{:S(2)}) collective-permute-start(bf16[288,768]{1,0:T(8,128)(2,1)S(1)} %constant_dynamic-update-slice_fusion.8), channel_id=1, source_target_pairs={{0,8},{4,12},{8,0},{12,4},{16,24},{20,28},{24,16},{28,20},{1,9},{5... | collective-permute-start | bytes 1327112 | tf_op jit(solution)/shard_map/ppermute | solution.py:56
  71.1 13.2 %collective-permute-start.20 = (bf16[288,768]{1,0:T(8,128)(2,1)S(1)}, bf16[288,768]{1,0:T(8,128)(2,1)S(1)}, u32[]{:S(2)}, u32[]{:S(2)}) collective-permute-start(bf16[288,768]{1,0:T(8,128)(2,1)S(1)} %constant_dynamic-update-slice_fusion.8), channel_id=1, source_target_pairs={{0,16},{4,20},{8,24},{12,28},{16,0},{20,4},{24,8},{28,12},{1,17},{... | collective-permute-start | bytes 1327112 | tf_op jit(solution)/shard_map/ppermute | solution.py:56
  72.8 16.3 %collective-permute-start.33 = (bf16[144,768]{1,0:T(8,128)(2,1)S(1)}, bf16[144,768]{1,0:T(8,128)(2,1)S(1)}, u32[]{:S(2)}, u32[]{:S(2)}) collective-permute-start(bf16[144,768]{1,0:T(8,128)(2,1)S(1)} %slice.538), channel_id=1, source_target_pairs={{0,16},{4,20},{8,24},{12,28},{16,0},{20,4},{24,8},{28,12},{1,17},{... | collective-permute-start | bytes 663560 | tf_op jit(solution)/shard_map/ppermute | solution.py:56
  73.4 22.4 %collective-permute-start.34 = (bf16[144,768]{1,0:T(8,128)(2,1)S(1)}, bf16[144,768]{1,0:T(8,128)(2,1)S(1)}, u32[]{:S(2)}, u32[]{:S(2)}) collective-permute-start(bf16[144,768]{1,0:T(8,128)(2,1)S(1)} %slice.539), channel_id=1, source_target_pairs={{0,8},{4,12},{8,0},{12,4},{16,24},{20,28},{24,16},{28,20},{1,9},{5... | collective-permute-start | bytes 663560 | tf_op jit(solution)/shard_map/ppermute | solution.py:56
  74.1 19.3 %collective-permute-start.8 = (bf16[144,768]{1,0:T(8,128)(2,1)S(1)}, bf16[144,768]{1,0:T(8,128)(2,1)S(1)}, u32[]{:S(2)}, u32[]{:S(2)}) collective-permute-start(bf16[144,768]{1,0:T(8,128)(2,1)S(1)} %slice.508), channel_id=1, source_target_pairs={{0,16},{4,20},{8,24},{12,28},{16,0},{20,4},{24,8},{28,12},{1,17},{... | collective-permute-start | bytes 663560 | tf_op jit(solution)/shard_map/ppermute | solution.py:56
  82.7 13.6 %collective-permute-start.9 = (bf16[144,768]{1,0:T(8,128)(2,1)S(1)}, bf16[144,768]{1,0:T(8,128)(2,1)S(1)}, u32[]{:S(2)}, u32[]{:S(2)}) collective-permute-start(bf16[144,768]{1,0:T(8,128)(2,1)S(1)} %slice.509), channel_id=1, source_target_pairs={{0,8},{4,12},{8,0},{12,4},{16,24},{20,28},{24,16},{28,20},{1,9},{5... | collective-permute-start | bytes 663560 | tf_op jit(solution)/shard_map/ppermute | solution.py:56
  98.8 15.6 %collective-permute-start.24 = (bf16[288,768]{1,0:T(8,128)(2,1)S(1)}, bf16[288,768]{1,0:T(8,128)(2,1)S(1)}, u32[]{:S(2)}, u32[]{:S(2)}) collective-permute-start(bf16[288,768]{1,0:T(8,128)(2,1)S(1)} %constant_dynamic-update-slice_fusion.11), channel_id=1, source_target_pairs={{0,4},{4,0},{8,12},{12,8},{16,20},{20,16},{24,28},{28,24},{1,5},{5... | collective-permute-start | bytes 1327112 | tf_op jit(solution)/shard_map/ppermute | solution.py:56
  175.2 92.4 %collective-permute-start.52 = (bf16[4,4,96,768]{3,2,1,0:T(8,128)(2,1)}, bf16[4,4,96,768]{3,2,1,0:T(8,128)(2,1)}, u32[]{:S(2)}, u32[]{:S(2)}) collective-permute-start(bf16[4,4,96,768]{3,2,1,0:T(8,128)(2,1)} %pad_maximum_fusion.9), channel_id=1, source_target_pairs={{0,4},{4,0},{8,12},{12,8},{16,20},{20,16},{24,28},{28,24},{1,5},{5... | collective-permute-start | bytes 7077896 | tf_op jit(solution)/shard_map/ppermute | solution.py:56
  179.9 87.8 %collective-permute-start.44 = (bf16[4,4,96,768]{3,2,1,0:T(8,128)(2,1)}, bf16[4,4,96,768]{3,2,1,0:T(8,128)(2,1)}, u32[]{:S(2)}, u32[]{:S(2)}) collective-permute-start(bf16[4,4,96,768]{3,2,1,0:T(8,128)(2,1)} %pad_maximum_fusion.8), channel_id=1, source_target_pairs={{0,4},{4,0},{8,12},{12,8},{16,20},{20,16},{24,28},{28,24},{1,5},{5... | collective-permute-start | bytes 7077896 | tf_op jit(solution)/shard_map/ppermute | solution.py:56
  199.6 43.3 %collective-permute-start.70 = (f32[1152]{0:T(1024)S(1)}, f32[1152]{0:T(1024)S(1)}, u32[]{:S(2)}, u32[]{:S(2)}) collective-permute-start(f32[1152]{0:T(1024)S(1)} %concatenate.115), channel_id=1, source_target_pairs={{0,1},{1,2},{2,3},{3,0},{4,5},{5,6},{6,7},{7,4},{8,9},{9,10},{10,1... | collective-permute-start | bytes 13832 | tf_op jit(solution)/shard_map/ppermute | solution.py:53
  209.1 33.8 %collective-permute-start.68 = (f32[1152]{0:T(1024)S(1)}, f32[1152]{0:T(1024)S(1)}, u32[]{:S(2)}, u32[]{:S(2)}) collective-permute-start(f32[1152]{0:T(1024)S(1)} %concatenate.113), channel_id=1, source_target_pairs={{0,3},{1,0},{2,1},{3,2},{4,7},{5,4},{6,5},{7,6},{8,11},{9,8},{10,9... | collective-permute-start | bytes 13832 | tf_op jit(solution)/shard_map/ppermute | solution.py:53
  209.3 33.6 %collective-permute-start.69 = (f32[1152]{0:T(1024)S(1)}, f32[1152]{0:T(1024)S(1)}, u32[]{:S(2)}, u32[]{:S(2)}) collective-permute-start(f32[1152]{0:T(1024)S(1)} %concatenate.114), channel_id=1, source_target_pairs={{0,2},{1,3},{2,0},{3,1},{4,6},{5,7},{6,4},{7,5},{8,10},{9,11},{10,... | collective-permute-start | bytes 13832 | tf_op jit(solution)/shard_map/ppermute | solution.py:53
  242.9 35.2 %collective-permute-start.36 = (bf16[4,4,96,768]{3,2,1,0:T(8,128)(2,1)}, bf16[4,4,96,768]{3,2,1,0:T(8,128)(2,1)}, u32[]{:S(2)}, u32[]{:S(2)}) collective-permute-start(bf16[4,4,96,768]{3,2,1,0:T(8,128)(2,1)} %pad_maximum_fusion.7), channel_id=1, source_target_pairs={{0,4},{4,0},{8,12},{12,8},{16,20},{20,16},{24,28},{28,24},{1,5},{5... | collective-permute-start | bytes 7077896 | tf_op jit(solution)/shard_map/ppermute | solution.py:56
  273.5 16.3 %collective-permute-start.53 = (bf16[2,2,96,768]{3,2,1,0:T(8,128)(2,1)S(1)}, bf16[2,2,96,768]{3,2,1,0:T(8,128)(2,1)S(1)}, u32[]{:S(2)}, u32[]{:S(2)}) collective-permute-start(bf16[2,2,96,768]{3,2,1,0:T(8,128)(2,1)S(1)} %pad_maximum_fusion.18), channel_id=1, source_target_pairs={{0,8},{4,12},{8,0},{12,4},{16,24},{20,28},{24,16},{28,20},{1,9},{5... | collective-permute-start | bytes 1769480 | tf_op jit(solution)/shard_map/ppermute | solution.py:56
  273.6 16.7 %collective-permute-start.56 = (bf16[2,2,96,768]{3,2,1,0:T(8,128)(2,1)S(1)}, bf16[2,2,96,768]{3,2,1,0:T(8,128)(2,1)S(1)}, u32[]{:S(2)}, u32[]{:S(2)}) collective-permute-start(bf16[2,2,96,768]{3,2,1,0:T(8,128)(2,1)S(1)} %pad_maximum_fusion.19), channel_id=1, source_target_pairs={{0,16},{4,20},{8,24},{12,28},{16,0},{20,4},{24,8},{28,12},{1,17},{... | collective-permute-start | bytes 1769480 | tf_op jit(solution)/shard_map/ppermute | solution.py:56
  274.3 28.1 %collective-permute-start.45 = (bf16[2,2,96,768]{3,2,1,0:T(8,128)(2,1)S(1)}, bf16[2,2,96,768]{3,2,1,0:T(8,128)(2,1)S(1)}, u32[]{:S(2)}, u32[]{:S(2)}) collective-permute-start(bf16[2,2,96,768]{3,2,1,0:T(8,128)(2,1)S(1)} %pad_maximum_fusion.16), channel_id=1, source_target_pairs={{0,8},{4,12},{8,0},{12,4},{16,24},{20,28},{24,16},{28,20},{1,9},{5... | collective-permute-start | bytes 1769480 | tf_op jit(solution)/shard_map/ppermute | solution.py:56
  276.5 26.1 %collective-permute-start.48 = (bf16[2,2,96,768]{3,2,1,0:T(8,128)(2,1)S(1)}, bf16[2,2,96,768]{3,2,1,0:T(8,128)(2,1)S(1)}, u32[]{:S(2)}, u32[]{:S(2)}) collective-permute-start(bf16[2,2,96,768]{3,2,1,0:T(8,128)(2,1)S(1)} %pad_maximum_fusion.17), channel_id=1, source_target_pairs={{0,16},{4,20},{8,24},{12,28},{16,0},{20,4},{24,8},{28,12},{1,17},{... | collective-permute-start | bytes 1769480 | tf_op jit(solution)/shard_map/ppermute | solution.py:56
  280.5 34.6 %collective-permute-start.37 = (bf16[2,2,96,768]{3,2,1,0:T(8,128)(2,1)S(1)}, bf16[2,2,96,768]{3,2,1,0:T(8,128)(2,1)S(1)}, u32[]{:S(2)}, u32[]{:S(2)}) collective-permute-start(bf16[2,2,96,768]{3,2,1,0:T(8,128)(2,1)S(1)} %pad_maximum_fusion.14), channel_id=1, source_target_pairs={{0,8},{4,12},{8,0},{12,4},{16,24},{20,28},{24,16},{28,20},{1,9},{5... | collective-permute-start | bytes 1769480 | tf_op jit(solution)/shard_map/ppermute | solution.py:56
  289.8 25.5 %collective-permute-start.40 = (bf16[2,2,96,768]{3,2,1,0:T(8,128)(2,1)S(1)}, bf16[2,2,96,768]{3,2,1,0:T(8,128)(2,1)S(1)}, u32[]{:S(2)}, u32[]{:S(2)}) collective-permute-start(bf16[2,2,96,768]{3,2,1,0:T(8,128)(2,1)S(1)} %pad_maximum_fusion.15), channel_id=1, source_target_pairs={{0,16},{4,20},{8,24},{12,28},{16,0},{20,4},{24,8},{28,12},{1,17},{... | collective-permute-start | bytes 1769480 | tf_op jit(solution)/shard_map/ppermute | solution.py:56
  290.4 31.2 %collective-permute-start.54 = (bf16[2,96,768]{2,1,0:T(8,128)(2,1)S(1)}, bf16[2,96,768]{2,1,0:T(8,128)(2,1)S(1)}, u32[]{:S(2)}, u32[]{:S(2)}) collective-permute-start(bf16[2,96,768]{2,1,0:T(8,128)(2,1)S(1)} %fusion.127), channel_id=1, source_target_pairs={{0,16},{4,20},{8,24},{12,28},{16,0},{20,4},{24,8},{28,12},{1,17},{... | collective-permute-start | bytes 884744 | tf_op jit(solution)/shard_map/ppermute | solution.py:56
  302.4 21.1 %collective-permute-start.57 = (bf16[2,96,768]{2,1,0:T(8,128)(2,1)S(1)}, bf16[2,96,768]{2,1,0:T(8,128)(2,1)S(1)}, u32[]{:S(2)}, u32[]{:S(2)}) collective-permute-start(bf16[2,96,768]{2,1,0:T(8,128)(2,1)S(1)} %fusion.126), channel_id=1, source_target_pairs={{0,8},{4,12},{8,0},{12,4},{16,24},{20,28},{24,16},{28,20},{1,9},{5... | collective-permute-start | bytes 884744 | tf_op jit(solution)/shard_map/ppermute | solution.py:56
  302.6 25.3 %collective-permute-start.46 = (bf16[2,96,768]{2,1,0:T(8,128)(2,1)S(1)}, bf16[2,96,768]{2,1,0:T(8,128)(2,1)S(1)}, u32[]{:S(2)}, u32[]{:S(2)}) collective-permute-start(bf16[2,96,768]{2,1,0:T(8,128)(2,1)S(1)} %fusion.132), channel_id=1, source_target_pairs={{0,16},{4,20},{8,24},{12,28},{16,0},{20,4},{24,8},{28,12},{1,17},{... | collective-permute-start | bytes 884744 | tf_op jit(solution)/shard_map/ppermute | solution.py:56
  315.1 13.4 %collective-permute-start.49 = (bf16[2,96,768]{2,1,0:T(8,128)(2,1)S(1)}, bf16[2,96,768]{2,1,0:T(8,128)(2,1)S(1)}, u32[]{:S(2)}, u32[]{:S(2)}) collective-permute-start(bf16[2,96,768]{2,1,0:T(8,128)(2,1)S(1)} %fusion.131), channel_id=1, source_target_pairs={{0,8},{4,12},{8,0},{12,4},{16,24},{20,28},{24,16},{28,20},{1,9},{5... | collective-permute-start | bytes 884744 | tf_op jit(solution)/shard_map/ppermute | solution.py:56
  315.2 16.5 %collective-permute-start.38 = (bf16[2,96,768]{2,1,0:T(8,128)(2,1)S(1)}, bf16[2,96,768]{2,1,0:T(8,128)(2,1)S(1)}, u32[]{:S(2)}, u32[]{:S(2)}) collective-permute-start(bf16[2,96,768]{2,1,0:T(8,128)(2,1)S(1)} %fusion.137), channel_id=1, source_target_pairs={{0,16},{4,20},{8,24},{12,28},{16,0},{20,4},{24,8},{28,12},{1,17},{... | collective-permute-start | bytes 884744 | tf_op jit(solution)/shard_map/ppermute | solution.py:56
  327.9 13.3 %collective-permute-start.58 = (bf16[96,768]{1,0:T(8,128)(2,1)S(1)}, bf16[96,768]{1,0:T(8,128)(2,1)S(1)}, u32[]{:S(2)}, u32[]{:S(2)}) collective-permute-start(bf16[96,768]{1,0:T(8,128)(2,1)S(1)} %get-tuple-element.119), channel_id=1, source_target_pairs={{0,2},{1,3},{2,0},{3,1},{4,6},{5,7},{6,4},{7,5},{8,10},{9,11},{10,... | collective-permute-start | bytes 442376 | tf_op jit(solution)/shard_map/ppermute | solution.py:53
  328.5 13.3 %collective-permute-start.55 = (bf16[96,768]{1,0:T(8,128)(2,1)S(1)}, bf16[96,768]{1,0:T(8,128)(2,1)S(1)}, u32[]{:S(2)}, u32[]{:S(2)}) collective-permute-start(bf16[96,768]{1,0:T(8,128)(2,1)S(1)} %slice_bitcast_fusion.39), channel_id=1, source_target_pairs={{0,3},{1,0},{2,1},{3,2},{4,7},{5,4},{6,5},{7,6},{8,11},{9,8},{10,9... | collective-permute-start | bytes 442376 | tf_op jit(solution)/shard_map/ppermute | solution.py:53
  331.8 17.9 %collective-permute-start.51 = (bf16[96,768]{1,0:T(8,128)(2,1)S(1)}, bf16[96,768]{1,0:T(8,128)(2,1)S(1)}, u32[]{:S(2)}, u32[]{:S(2)}) collective-permute-start(bf16[96,768]{1,0:T(8,128)(2,1)S(1)} %get-tuple-element.118), channel_id=1, source_target_pairs={{0,1},{1,2},{2,3},{3,0},{4,5},{5,6},{6,7},{7,4},{8,9},{9,10},{10,1... | collective-permute-start | bytes 442376 | tf_op jit(solution)/shard_map/ppermute | solution.py:53
  331.8 21.6 %collective-permute-start.50 = (bf16[96,768]{1,0:T(8,128)(2,1)S(1)}, bf16[96,768]{1,0:T(8,128)(2,1)S(1)}, u32[]{:S(2)}, u32[]{:S(2)}) collective-permute-start(bf16[96,768]{1,0:T(8,128)(2,1)S(1)} %get-tuple-element.117), channel_id=1, source_target_pairs={{0,2},{1,3},{2,0},{3,1},{4,6},{5,7},{6,4},{7,5},{8,10},{9,11},{10,... | collective-permute-start | bytes 442376 | tf_op jit(solution)/shard_map/ppermute | solution.py:53
  333.7 19.7 %collective-permute-start.47 = (bf16[96,768]{1,0:T(8,128)(2,1)S(1)}, bf16[96,768]{1,0:T(8,128)(2,1)S(1)}, u32[]{:S(2)}, u32[]{:S(2)}) collective-permute-start(bf16[96,768]{1,0:T(8,128)(2,1)S(1)} %slice_bitcast_fusion.43), channel_id=1, source_target_pairs={{0,3},{1,0},{2,1},{3,2},{4,7},{5,4},{6,5},{7,6},{8,11},{9,8},{10,9... | collective-permute-start | bytes 442376 | tf_op jit(solution)/shard_map/ppermute | solution.py:53
  341.8 18.5 %collective-permute-start.42 = (bf16[96,768]{1,0:T(8,128)(2,1)S(1)}, bf16[96,768]{1,0:T(8,128)(2,1)S(1)}, u32[]{:S(2)}, u32[]{:S(2)}) collective-permute-start(bf16[96,768]{1,0:T(8,128)(2,1)S(1)} %get-tuple-element.115), channel_id=1, source_target_pairs={{0,2},{1,3},{2,0},{3,1},{4,6},{5,7},{6,4},{7,5},{8,10},{9,11},{10,... | collective-permute-start | bytes 442376 | tf_op jit(solution)/shard_map/ppermute | solution.py:53
  360.4 16.0 %collective-permute-start.60 = (bf16[288,768]{1,0:T(8,128)(2,1)S(1)}, bf16[288,768]{1,0:T(8,128)(2,1)S(1)}, u32[]{:S(2)}, u32[]{:S(2)}) collective-permute-start(bf16[288,768]{1,0:T(8,128)(2,1)S(1)} %pad_maximum_fusion.20), channel_id=1, source_target_pairs={{0,4},{4,0},{8,12},{12,8},{16,20},{20,16},{24,28},{28,24},{1,5},{5... | collective-permute-start | bytes 1327112 | tf_op jit(solution)/shard_map/ppermute | solution.py:56
  360.5 12.6 %collective-permute-start.61 = (bf16[288,768]{1,0:T(8,128)(2,1)S(1)}, bf16[288,768]{1,0:T(8,128)(2,1)S(1)}, u32[]{:S(2)}, u32[]{:S(2)}) collective-permute-start(bf16[288,768]{1,0:T(8,128)(2,1)S(1)} %pad_maximum_fusion.20), channel_id=1, source_target_pairs={{0,8},{4,12},{8,0},{12,4},{16,24},{20,28},{24,16},{28,20},{1,9},{5... | collective-permute-start | bytes 1327112 | tf_op jit(solution)/shard_map/ppermute | solution.py:56
  360.9 14.6 %collective-permute-start.63 = (bf16[288,768]{1,0:T(8,128)(2,1)S(1)}, bf16[288,768]{1,0:T(8,128)(2,1)S(1)}, u32[]{:S(2)}, u32[]{:S(2)}) collective-permute-start(bf16[288,768]{1,0:T(8,128)(2,1)S(1)} %pad_maximum_fusion.20), channel_id=1, source_target_pairs={{0,16},{4,20},{8,24},{12,28},{16,0},{20,4},{24,8},{28,12},{1,17},{... | collective-permute-start | bytes 1327112 | tf_op jit(solution)/shard_map/ppermute | solution.py:56
  (89 other events, 610.8 us)
